TPU v7x, 32 devices: a whole 2x2x4 slice. The times are simulated.
32 devices in a mesh: dp: 2 (over x), seq: 16 (over z, y, core).
Axes of the slice: x: 2, y: 2, z: 4, core: 2. Of those that a mesh axis runs over, the one named last changes fastest.
Arguments:
- query: bfloat16 [2048, 3072], P('seq', 'dp'), may hold values from -300 to 300
- key: bfloat16 [2048, 3072], P('seq', 'dp'), may hold values from -10 to 10
- value: bfloat16 [2048, 3072], P('seq', 'dp'), may hold values from -6 to 6
- d_query: bfloat16 [2048, 3072], P('seq', 'dp'), may hold values from -6 to 6
- d_key: bfloat16 [2048, 3072], P('seq', 'dp'), may hold values from -6 to 6
- d_value: bfloat16 [2048, 3072], P('seq', 'dp'), may hold values from -6 to 6
- residual: bfloat16 [2048, 3072], P('seq', 'dp'), may hold values from -6 to 6
- d_residual: bfloat16 [2048, 3072], P('seq', 'dp'), may hold values from -6 to 6
- w_in: bfloat16 [3072, 7168], P('seq', 'dp'), may hold values from -0.109375 to 0.109375
- w_out: bfloat16 [7168, 3072], P(('dp', 'seq')), may hold values from -0.125 to 0.125
Outputs:
- block_out: bfloat16 [2048, 3072], P('seq', 'dp')
- d_block_out: bfloat16 [2048, 3072], P('seq', 'dp')
All inputs are finite; a program needn't handle non-finite values.
Results may differ from a plain program's by a relative error of at most 0.025.
Values may be sent and summed in bfloat16 or wider, within the bound.
A program may use at most 192 MiB of HBM per device.

v0:
```python
import math

import jax
import jax.numpy as jnp
from jax import lax
from jax.sharding import PartitionSpec as P

HEAD_DIM = 128


gelu_coeff = 0.7978845608
cubic_coeff = 0.044715


def gelu_pair(pre_act, d_pre_act):
    inner_arg = gelu_coeff * (pre_act + cubic_coeff * pre_act * pre_act * pre_act)
    hyper = jnp.tanh(inner_arg)
    gelu_value = 0.5 * pre_act * (1.0 + hyper)
    gelu_slope = 0.5 * (1.0 + hyper) + 0.5 * pre_act * (1.0 - hyper * hyper) * gelu_coeff * (
        1.0 + 3.0 * cubic_coeff * pre_act * pre_act
    )
    return (gelu_value, gelu_slope * d_pre_act)


def on_device(query, key, value, d_query, d_key, d_value, residual, d_residual, w_in, w_out):
    row_count = query.shape[0]
    feat_width = query.shape[1]
    head_count = feat_width // HEAD_DIM
    score_scale = 1.0 / math.sqrt(HEAD_DIM)
    query_heads = query.reshape(row_count, head_count, HEAD_DIM)
    dquery_heads = d_query.reshape(row_count, head_count, HEAD_DIM)
    pieces = (
        lax.all_gather(key, "seq", axis=0, tiled=True),
        lax.all_gather(value, "seq", axis=0, tiled=True),
        lax.all_gather(d_key, "seq", axis=0, tiled=True),
        lax.all_gather(d_value, "seq", axis=0, tiled=True),
    )
    run_peak = jnp.full((head_count, row_count), -1e30, jnp.float32)
    key_heads, value_heads, dkey_heads, dvalue_heads = tuple(
        (piece.reshape(piece.shape[0], head_count, HEAD_DIM) for piece in pieces)
    )
    scores = (
        jnp.einsum("qhd,khd->hqk", query_heads, key_heads, preferred_element_type=jnp.float32)
        * score_scale
    )
    d_scores = (
        jnp.einsum("qhd,khd->hqk", dquery_heads, key_heads, preferred_element_type=jnp.float32)
        + jnp.einsum("qhd,khd->hqk", query_heads, dkey_heads, preferred_element_type=jnp.float32)
    ) * score_scale
    new_peak = jnp.maximum(run_peak, jnp.max(scores, axis=2))
    weights = jnp.exp(scores - new_peak[:, :, None])
    mixed = weights * d_scores
    weights_low = weights.astype(jnp.bfloat16)
    mixed_low = mixed.astype(jnp.bfloat16)
    new_total = jnp.sum(weights, axis=2)
    new_slope = jnp.sum(mixed, axis=2)
    new_accum = jnp.einsum(
        "hqk,khd->hqd", weights_low, value_heads, preferred_element_type=jnp.float32
    )
    new_tangent = jnp.einsum(
        "hqk,khd->hqd", mixed_low, value_heads, preferred_element_type=jnp.float32
    ) + jnp.einsum("hqk,khd->hqd", weights_low, dvalue_heads, preferred_element_type=jnp.float32)
    attended = new_accum / new_total[:, :, None]
    d_attended = (
        new_tangent / new_total[:, :, None] - (new_slope / new_total)[:, :, None] * attended
    )
    attended = attended.transpose(1, 0, 2).reshape(row_count, feat_width)
    d_attended = d_attended.transpose(1, 0, 2).reshape(row_count, feat_width)
    mixed_in = (residual.astype(jnp.float32) + attended).astype(jnp.bfloat16)
    d_mixed_in = (d_residual.astype(jnp.float32) + d_attended).astype(jnp.bfloat16)
    w_in_whole, w_out_whole = (
        lax.all_gather(w_in, "seq", axis=0, tiled=True),
        lax.all_gather(w_out, "seq", axis=0, tiled=True),
    )
    whole_in, d_whole_in = (
        lax.all_gather(mixed_in, "dp", axis=1, tiled=True),
        lax.all_gather(d_mixed_in, "dp", axis=1, tiled=True),
    )
    pre_act = jnp.dot(whole_in, w_in_whole, preferred_element_type=jnp.float32)
    d_pre_act = jnp.dot(d_whole_in, w_in_whole, preferred_element_type=jnp.float32)
    hidden, d_hidden = gelu_pair(pre_act, d_pre_act)
    hidden = hidden.astype(jnp.bfloat16)
    d_hidden = d_hidden.astype(jnp.bfloat16)
    partial_value = jnp.dot(hidden, w_out_whole, preferred_element_type=jnp.float32)
    d_partial = jnp.dot(d_hidden, w_out_whole, preferred_element_type=jnp.float32)
    summed, d_summed = (
        lax.psum_scatter(
            partial_value.astype(jnp.bfloat16), "dp", scatter_dimension=1, tiled=True
        ).astype(jnp.float32),
        lax.psum_scatter(
            d_partial.astype(jnp.bfloat16), "dp", scatter_dimension=1, tiled=True
        ).astype(jnp.float32),
    )
    block_out = (mixed_in.astype(jnp.float32) + summed).astype(jnp.bfloat16)
    d_block_out = (d_mixed_in.astype(jnp.float32) + d_summed).astype(jnp.bfloat16)
    return (block_out, d_block_out)


def solution(mesh):
    in_specs = (
        P("seq", "dp"),
        P("seq", "dp"),
        P("seq", "dp"),
        P("seq", "dp"),
        P("seq", "dp"),
        P("seq", "dp"),
        P("seq", "dp"),
        P("seq", "dp"),
        P("seq", "dp"),
        P(("dp", "seq"), None),
    )
    out_specs = (P("seq", "dp"), P("seq", "dp"))
    return jax.shard_map(
        on_device, mesh=mesh, in_specs=in_specs, out_specs=out_specs, check_vma=False
    )
```

profile of v0, /device:TPU:8, one launch (start us, length us, event | category | flops | bytes accessed | tf_op | source)
XLA Modules:
  0.0 554.2 jit_solution(12770551989080818743)
XLA Ops:
  8.7 1.9 copy.20
  10.7 1.9 copy.28
  13.8 1.2 copy.19
  15.3 57.6 %all-gather.9.cloned.1.call-done = bf16[2048,1536]{1,0:T(8,128)(2,1)} async-done(((bf16[128,1536]{1,0:T(8,128)(2,1)}), bf16[2048,1536]{1,0:T(8,128)(2,1)}) %all-gather.9.cloned.1.call-update) | async-done | bytes 6291472 | tf_op jit(solution)/shard_map/all_gather | solution.py:34
  72.9 8.7 %copy.23 = bf16[2048,1536]{0,1:T(8,128)(2,1)} copy(bf16[2048,1536]{1,0:T(8,128)(2,1)} %all-gather.9.cloned.1.call-done) | data formatting | bytes 12582912 | tf_op jit(solution)/shard_map/all_gather | solution.py:34
  81.6 53.7 %all-gather.17.cloned.1.call-done = bf16[2048,1536]{1,0:T(8,128)(2,1)} async-done(((bf16[128,1536]{1,0:T(8,128)(2,1)}), bf16[2048,1536]{1,0:T(8,128)(2,1)}) %all-gather.17.cloned.1.call-update) | async-done | bytes 6291472 | tf_op jit(solution)/shard_map/all_gather | solution.py:36
  135.3 8.7 %copy.31 = bf16[2048,1536]{0,1:T(8,128)(2,1)} copy(bf16[2048,1536]{1,0:T(8,128)(2,1)} %all-gather.17.cloned.1.call-done) | data formatting | bytes 12582912 | tf_op jit(solution)/shard_map/all_gather | solution.py:36
  144.0 56.1 %all-gather.7.cloned.1.call-done = bf16[2048,1536]{0,1:T(8,128)(2,1)} async-done(((bf16[128,1536]{0,1:T(8,128)(2,1)}), bf16[2048,1536]{0,1:T(8,128)(2,1)}) %all-gather.7.cloned.1.call-update) | async-done | bytes 6291472 | tf_op jit(solution)/shard_map/all_gather | solution.py:33
  200.2 4.9 multiply_reduce_fusion
  205.1 6.8 %fusion.38 = f32[12,128,2048]{2,1,0:T(8,128)} fusion(bf16[128,12,128]{0,2,1:T(8,128)(2,1)S(1)} %bitcast.51, bf16[2048,12,128]{0,2,1:T(8,128)(2,1)S(1)} %bitcast.42), kind=kOutput, calls=%fused_computation.44 | convolution fusion | flops 805306368 | bytes 19267584 | tf_op jit(solution)/shard_map/qhd,khd->hqk/dot_general | solution.py:47
  211.9 1.5 copy-done
  213.4 2.4 fusion
  215.8 50.4 %all-gather.15.cloned.1.call-done = bf16[2048,1536]{0,1:T(8,128)(2,1)} async-done(((bf16[128,1536]{0,1:T(8,128)(2,1)}), bf16[2048,1536]{0,1:T(8,128)(2,1)}) %all-gather.15.cloned.1.call-update) | async-done | bytes 6291472 | tf_op jit(solution)/shard_map/all_gather | solution.py:35
  266.2 15.8 %fusion.36 = (f32[12,128]{1,0:T(8,128)S(1)}, bf16[12,128,2048]{2,1,0:T(8,128)(2,1)}) fusion(f32[12,128,2048]{2,1,0:T(8,128)} %fusion.38, bf16[128,12,128]{0,2,1:T(8,128)(2,1)S(1)} %bitcast.50, bf16[2048,12,128]{0,2,1:T(8,128)(2,1)} %bitcast.48, f32[12,128]{1,0:T(8,128)S(1)} %broadcast_maximum_fusion, f32[12,128,2048]{2,1,0:T(8,128)} %copy-done), kind=kOutput, calls=%fused_computation.42 | convolution fusion | flops 827324928 | bytes 38154240 | tf_op jit(solution)/shard_map/qhd,khd->hqk/dot_general | solution.py:48
  282.0 6.5 %fusion.27 = f32[12,128,128]{1,2,0:T(8,128)S(1)} fusion(bf16[2048,12,128]{0,2,1:T(8,128)(2,1)S(1)} %bitcast.45, f32[12,128,2048]{2,1,0:T(8,128)} %copy-done, f32[12,128]{1,0:T(8,128)S(1)} %broadcast_maximum_fusion), kind=kOutput, calls=%fused_computation.29 | convolution fusion | flops 814743552 | bytes 19666944 | tf_op jit(solution)/shard_map/hqk,khd->hqd/dot_general | solution.py:62
  288.5 10.4 %fusion.22 = f32[128,12,128]{0,2,1:T(8,128)} fusion(bf16[2048,12,128]{0,2,1:T(8,128)(2,1)} %bitcast.46, f32[12,128,2048]{2,1,0:T(8,128)} %copy-done, f32[12,128]{1,0:T(8,128)S(1)} %broadcast_maximum_fusion, f32[128,12]{0,1:T(8,128)S(1)} %bitcast.54), kind=kOutput, calls=%fused_computation.24 | convolution fusion | flops 814940160 | bytes 19673088 | tf_op jit(solution)/shard_map/hqk,khd->hqd/dot_general | solution.py:57
  298.9 6.2 %fusion.19 = f32[128,12,128]{0,2,1:T(8,128)} fusion(f32[12,128,128]{1,2,0:T(8,128)S(1)} %fusion.27, bf16[2048,12,128]{0,2,1:T(8,128)(2,1)} %bitcast.47, bf16[12,128,2048]{2,1,0:T(8,128)(2,1)S(1)} %copy-done.2, f32[128,12,128]{0,2,1:T(8,128)} %fusion.22, f32[128,12]{0,1:T(8,128)S(1)} %bitcast_divide_fusion, f32[128,12]{0,1:T(8,128)S(1)} %bitcast.55), kind=kOutput, calls=%fused_computation.23 | convolution fusion | flops 806092800 | bytes 14954496 | tf_op jit(solution)/shard_map/hqk,khd->hqd/dot_general | solution.py:60
  305.1 1.4 copy.32
  306.5 1.5 copy.24
  308.1 11.8 %all_gather.31 = bf16[128,3072]{1,0:T(8,128)(2,1)} all-gather(bf16[128,1536]{1,0:T(8,128)(2,1)S(1)} %add_convert_fusion.1), channel_id=1, replica_groups=mesh['dp'=2,'seq'=16] {'dp'}, dimensions={1}, use_global_device_ids=true | all-gather | bytes 1179648 | tf_op jit(solution)/shard_map/all_gather | solution.py:77
  320.0 10.8 %all_gather.26 = bf16[128,3072]{1,0:T(8,128)(2,1)S(1)} all-gather(bf16[128,1536]{1,0:T(8,128)(2,1)S(1)} %add_convert_fusion.3), channel_id=1, replica_groups=mesh['dp'=2,'seq'=16] {'dp'}, dimensions={1}, use_global_device_ids=true | all-gather | bytes 1179648 | tf_op jit(solution)/shard_map/all_gather | solution.py:76
  330.8 50.6 %all-gather.11.cloned.1.call-done = bf16[3072,3584]{1,0:T(8,128)(2,1)} async-done(((bf16[192,3584]{1,0:T(8,128)(2,1)}), bf16[3072,3584]{1,0:T(8,128)(2,1)}) %all-gather.11.cloned.1.call-update) | async-done | bytes 22020112 | tf_op jit(solution)/shard_map/all_gather | solution.py:72
  381.4 11.7 %fusion.37 = f32[128,3584]{1,0:T(8,128)} fusion(bf16[128,3072]{1,0:T(8,128)(2,1)S(1)} %all_gather.26, bf16[3072,3584]{1,0:T(8,128)(2,1)} %all-gather.11.cloned.1.call-done), kind=kOutput, calls=%fused_computation.43 | convolution fusion | flops 2818572288 | bytes 24641536 | tf_op jit(solution)/shard_map/dot_general | solution.py:79
  393.1 3.4 copy-done.1
  396.5 6.5 %fusion.4 = bf16[128,3584]{1,0:T(8,128)(2,1)} fusion(bf16[128,3072]{1,0:T(8,128)(2,1)} %all_gather.31, bf16[3072,3584]{1,0:T(8,128)(2,1)S(1)} %copy-done.1, f32[128,3584]{1,0:T(8,128)} %fusion.37), kind=kOutput, calls=%fused_computation.8 | convolution fusion | flops 2827288576 | bytes 25559040 | tf_op jit(solution)/shard_map/dot_general | solution.py:80
  403.0 93.5 %all-gather.13.cloned.1.call-done = bf16[3584,3072]{1,0:T(8,128)(2,1)} async-done(((bf16[224,3072]{1,0:T(8,128)(2,1)}), bf16[3584,3072]{1,0:T(8,128)(2,1)}) %all-gather.13.cloned.1.call-update) | async-done | bytes 22020112 | tf_op jit(solution)/shard_map/all_gather | solution.py:73
  496.6 11.5 %convolution_convert_fusion = bf16[128,3072]{1,0:T(8,128)(2,1)} fusion(bf16[128,3584]{1,0:T(8,128)(2,1)} %fusion.4, bf16[3584,3072]{1,0:T(8,128)(2,1)} %all-gather.13.cloned.1.call-done), kind=kOutput, calls=%fused_computation.9 | convolution fusion | flops 2818965504 | bytes 23724032 | tf_op jit(solution)/shard_map/dot_general | solution.py:85
  508.2 11.7 %convolution_convert_fusion.1 = bf16[128,3072]{1,0:T(8,128)(2,1)} fusion(bf16[3584,3072]{1,0:T(8,128)(2,1)} %all-gather.13.cloned.1.call-done, f32[128,3584]{1,0:T(8,128)S(1)} %copy-done.3), kind=kOutput, calls=%fused_computation.10 | convolution fusion | flops 2823094272 | bytes 24641536 | tf_op jit(solution)/shard_map/dot_general | solution.py:84
  519.8 5.9 %reduce-scatter.5.cloned.1.call-done = bf16[128,1536]{1,0:T(8,128)(2,1)} async-done(((bf16[128,3072]{1,0:T(8,128)(2,1)}), bf16[128,1536]{1,0:T(8,128)(2,1)}) %reduce-scatter.5.cloned.1.call-update) | async-done | bytes 393232 | tf_op jit(solution)/shard_map/reduce_scatter | solution.py:90
  525.7 1.8 add_convert_fusion
  527.6 18.0 %reduce-scatter.3.cloned.1.call-done = bf16[128,1536]{1,0:T(8,128)(2,1)} async-done(((bf16[128,3072]{1,0:T(8,128)(2,1)}), bf16[128,1536]{1,0:T(8,128)(2,1)}) %reduce-scatter.3.cloned.1.call-update) | async-done | bytes 393232 | tf_op jit(solution)/shard_map/reduce_scatter | solution.py:87
  545.6 1.8 add_convert_fusion.2
  (43 shorter events, 3.2 us)
Async XLA Ops:
  7.2 7.9 %copy-start.4 = (bf16[128,1536]{1,0:T(8,128)(2,1)S(1)}, bf16[128,1536]{1,0:T(8,128)(2,1)}, u32[]{:S(2)}) copy-start(bf16[128,1536]{1,0:T(8,128)(2,1)} %param.13) | copy-start | bytes 1179652
  7.2 65.7 %all-gather.9.cloned.1.call-start = ((), (), s32[]{:S(2)}) async-start(), calls=%async_computation.3 | async-start | bytes 6684672 | tf_op jit(solution)/shard_map/all_gather | solution.py:34
  7.9 127.4 %all-gather.17.cloned.1.call-start = ((), (), s32[]{:S(2)}) async-start(), calls=%async_computation.8 | async-start | bytes 6684672 | tf_op jit(solution)/shard_map/all_gather | solution.py:36
  8.7 191.5 %all-gather.7.cloned.1.call-start = ((), (), s32[]{:S(2)}) async-start(), calls=%async_computation.2 | async-start | bytes 6684672 | tf_op jit(solution)/shard_map/all_gather | solution.py:33
  10.6 255.6 %all-gather.15.cloned.1.call-start = ((), (), s32[]{:S(2)}) async-start(), calls=%async_computation.7 | async-start | bytes 6684672 | tf_op jit(solution)/shard_map/all_gather | solution.py:35
  12.6 368.8 %all-gather.11.cloned.1.call-start = ((), (), s32[]{:S(2)}) async-start(), calls=%async_computation.4 | async-start | bytes 23396352 | tf_op jit(solution)/shard_map/all_gather | solution.py:72
  13.2 483.4 %all-gather.13.cloned.1.call-start = ((), (), s32[]{:S(2)}) async-start(), calls=%async_computation.5 | async-start | bytes 23396352 | tf_op jit(solution)/shard_map/all_gather | solution.py:73
  13.8 511.9 %reduce-scatter.5.cloned.1.call-start = ((), (), s32[]{:S(2)}) async-start(), calls=%async_computation.9 | async-start | bytes 1179648 | tf_op jit(solution)/shard_map/reduce_scatter | solution.py:90
  200.1 4.9 slice-start
  200.1 4.9 slice-start.1
  205.0 8.4 %copy-start = (f32[12,128,2048]{2,1,0:T(8,128)}, f32[12,128,2048]{2,1,0:T(8,128)S(1)}, u32[]{:S(2)}) copy-start(f32[12,128,2048]{2,1,0:T(8,128)S(1)} %get-tuple-element.3) | copy-start | bytes 37748740
  213.4 68.6 %slice-start.2 = ((s8[6291456]{0:T(1024)(128)(4,1)}), s8[2097152]{0:T(1024)(128)(4,1)S(1)}, s32[]{:S(2)}) async-start(s8[6291456]{0:T(1024)(128)(4,1)} %bitcast.43), calls=%async_computation.12 | async-start | bytes 4194304
  266.2 15.8 %slice-start.3 = ((s8[6291456]{0:T(1024)(128)(4,1)}), s8[4194304]{0:T(1024)(128)(4,1)S(1)}, s32[]{:S(2)}) async-start(s8[6291456]{0:T(1024)(128)(4,1)} %bitcast.43), calls=%async_computation.13 | async-start | bytes 8388608
  288.5 10.4 %copy-start.2 = (bf16[12,128,2048]{2,1,0:T(8,128)(2,1)S(1)}, bf16[12,128,2048]{2,1,0:T(8,128)(2,1)}, u32[]{:S(2)}) copy-start(bf16[12,128,2048]{2,1,0:T(8,128)(2,1)} %get-tuple-element.5) | copy-start | bytes 18874372
  298.9 9.1 %copy-start.5 = (bf16[128,1536]{1,0:T(8,128)(2,1)S(1)}, bf16[128,1536]{1,0:T(8,128)(2,1)}, u32[]{:S(2)}) copy-start(bf16[128,1536]{1,0:T(8,128)(2,1)} %param.17) | copy-start | bytes 1179652
  298.9 21.0 %copy-start.6 = (bf16[128,1536]{1,0:T(8,128)(2,1)S(1)}, bf16[128,1536]{1,0:T(8,128)(2,1)}, u32[]{:S(2)}) copy-start(bf16[128,1536]{1,0:T(8,128)(2,1)} %param.16) | copy-start | bytes 1179652
  381.4 15.1 %copy-start.1 = (bf16[3072,3584]{1,0:T(8,128)(2,1)S(1)}, bf16[3072,3584]{1,0:T(8,128)(2,1)}, u32[]{:S(2)}) copy-start(bf16[3072,3584]{1,0:T(8,128)(2,1)} %all-gather.11.cloned.1.call-done) | copy-start | bytes 66060292
  403.0 105.1 %copy-start.3 = (f32[128,3584]{1,0:T(8,128)S(1)}, f32[128,3584]{1,0:T(8,128)}, u32[]{:S(2)}) copy-start(f32[128,3584]{1,0:T(8,128)} %fusion.37) | copy-start | bytes 5505028
  508.1 37.5 %reduce-scatter.3.cloned.1.call-start = ((), (), s32[]{:S(2)}) async-start(), calls=%async_computation.6 | async-start | bytes 1179648 | tf_op jit(solution)/shard_map/reduce_scatter | solution.py:87
Sparse Core Ops, SparseCore 0:
  10.3 62.5 all-gather.8
  75.2 60.0 all-gather.16
  138.0 62.0 all-gather.6
  202.7 63.4 all-gather.14
  267.6 113.7 all-gather.10
  382.9 113.6 all-gather.12
  508.2 17.4 reduce-scatter.4
  528.0 17.5 reduce-scatter.2
where the time goes:
time: 557 us; the launch traced here: 554 us
  waiting for transfers between devices  388 us (70%)
  matrix products  91.9 us (16%)
  local copies, waits for them, and re-layouts  30.5 us (5%)
  blocking collectives  22.6 us (4%)
  between operations  14.3 us (3%)
  other arithmetic  6.27 us (1%)
    all_gather x1, waiting for transfers between devices, on_device(): lax.all_gather(w_out, 'seq', axis=0, tiled=True)  93.5 us
    all_gather x1, waiting for transfers between devices, on_device(): lax.all_gather(value, 'seq', axis=0, tiled=True)  57.6 us
    all_gather x1, waiting for transfers between devices, on_device(): lax.all_gather(key, 'seq', axis=0, tiled=True)  56.1 us
    all_gather x1, waiting for transfers between devices, on_device(): lax.all_gather(d_value, 'seq', axis=0, tiled=True)  53.7 us
    all_gather x1, waiting for transfers between devices, on_device(): lax.all_gather(w_in, 'seq', axis=0, tiled=True)  50.6 us
    all_gather x1, waiting for transfers between devices, on_device(): lax.all_gather(d_key, 'seq', axis=0, tiled=True)  50.4 us
    reduce_scatter x1, waiting for transfers between devices, on_device(): lax.psum_scatter(partial_value.astype(jnp.bfloat16), 'dp', scatter_dimens...  18 us
    dot_general x1, matrix products, on_device(): jnp.einsum('qhd,khd->hqk', query_heads, dkey_heads, preferred_element_typ...  15.8 us
  transfers between devices with their start and end apart: 8, of which 8 were waited for; matrix products, arithmetic and copies ran while one was open for 20% of the time, Pallas kernels for 0%

commit v1 on v0

v1 whole, which is shorter than its diff:
```python
import functools
import math

import jax
import jax.numpy as jnp
from jax import lax
from jax.experimental import pallas as pl
from jax.experimental.pallas import tpu as pltpu
from jax.sharding import PartitionSpec as P

HEAD_DIM = 128


gelu_coeff = 0.7978845608
cubic_coeff = 0.044715


def gelu_pair(pre_act, d_pre_act):
    inner_arg = gelu_coeff * (pre_act + cubic_coeff * pre_act * pre_act * pre_act)
    hyper = jnp.tanh(inner_arg)
    gelu_value = 0.5 * pre_act * (1.0 + hyper)
    gelu_slope = 0.5 * (1.0 + hyper) + 0.5 * pre_act * (1.0 - hyper * hyper) * gelu_coeff * (
        1.0 + 3.0 * cubic_coeff * pre_act * pre_act
    )
    return (gelu_value, gelu_slope * d_pre_act)


def nt(a, b):
    return lax.dot_general(a, b, (((1,), (1,)), ((), ())), preferred_element_type=jnp.float32)


def attend_kernel(q, dq, res, dres, k, v, dk, dv, out, *, rows):
    scale = 1.0 / math.sqrt(HEAD_DIM)
    keys = k[...]
    keys_pair = jnp.concatenate([keys, dk[...]], axis=1)
    values = v[...]
    values_pair = jnp.concatenate([values, dv[...]], axis=1)
    for start in range(0, q.shape[0], rows):
        part = pl.ds(start, rows)
        scores = nt(q[part, :], keys) * scale
        d_scores = nt(jnp.concatenate([dq[part, :], q[part, :]], axis=1), keys_pair) * scale
        peak = jnp.max(scores, axis=1, keepdims=True)
        weights = jnp.exp(scores - peak)
        mixed = weights * d_scores
        total = jnp.sum(weights, axis=1, keepdims=True)
        slope = jnp.sum(mixed, axis=1, keepdims=True)
        both = jnp.dot(
            weights.astype(jnp.bfloat16), values_pair, preferred_element_type=jnp.float32
        )
        tangent = both[:, HEAD_DIM:] + jnp.dot(
            mixed.astype(jnp.bfloat16), values, preferred_element_type=jnp.float32
        )
        attended = both[:, :HEAD_DIM] / total
        d_attended = tangent / total - (slope / total) * attended
        out[0, part, :] = (res[part, :].astype(jnp.float32) + attended).astype(jnp.bfloat16)
        out[1, part, :] = (dres[part, :].astype(jnp.float32) + d_attended).astype(jnp.bfloat16)


def attend(query, d_query, residual, d_residual, kv):
    rows, feats = query.shape
    heads = feats // HEAD_DIM
    length = kv.shape[0]
    own = pl.BlockSpec((rows, HEAD_DIM), lambda h: (0, h))

    def kv_spec(i):
        return pl.BlockSpec((length, HEAD_DIM), lambda h: (0, i * heads + h))

    return pl.pallas_call(
        functools.partial(attend_kernel, rows=min(rows, 128)),
        grid=(heads,),
        in_specs=[own] * 4 + [kv_spec(i) for i in range(4)],
        out_specs=pl.BlockSpec((2, rows, HEAD_DIM), lambda h: (0, 0, h)),
        out_shape=jax.ShapeDtypeStruct((2, rows, feats), jnp.bfloat16),
        cost_estimate=pl.CostEstimate(
            flops=12 * rows * length * feats, bytes_accessed=8 * length * feats, transcendentals=0
        ),
        name="attend",
    )(query, d_query, residual, d_residual, kv, kv, kv, kv)


def on_device(query, key, value, d_query, d_key, d_value, residual, d_residual, w_in, w_out):
    rows, feats = query.shape
    kv = lax.all_gather(
        jnp.concatenate([key, value, d_key, d_value], axis=1), "seq", axis=0, tiled=True
    )
    w_in_whole = lax.all_gather(w_in, "seq", axis=0, tiled=True)
    w_out_whole = lax.all_gather(w_out, "seq", axis=0, tiled=True)
    mixed = attend(query, d_query, residual, d_residual, kv).reshape(2 * rows, feats)
    whole = lax.all_gather(mixed, "dp", axis=1, tiled=True)
    pre = jnp.dot(whole, w_in_whole, preferred_element_type=jnp.float32)
    hidden, d_hidden = gelu_pair(pre[:rows], pre[rows:])
    hidden = jnp.concatenate([hidden.astype(jnp.bfloat16), d_hidden.astype(jnp.bfloat16)], axis=0)
    partial = jnp.dot(hidden, w_out_whole, preferred_element_type=jnp.float32)
    summed = lax.psum_scatter(
        partial.astype(jnp.bfloat16), "dp", scatter_dimension=1, tiled=True
    ).astype(jnp.float32)
    out = (mixed.astype(jnp.float32) + summed).astype(jnp.bfloat16)
    return (out[:rows], out[rows:])


def solution(mesh):
    in_specs = (P("seq", "dp"),) * 9 + (P(("dp", "seq"), None),)
    out_specs = (P("seq", "dp"), P("seq", "dp"))
    return jax.shard_map(
        on_device, mesh=mesh, in_specs=in_specs, out_specs=out_specs, check_vma=False
    )
```

time: 557 us -> 448 us (0.80)
  matrix products: 91.9 us -> 22.6 us
  local copies, waits for them, and re-layouts: 30.5 us -> 0.93 us
  blocking collectives: 22.6 us -> 0 us
  Pallas kernels: 0 us -> 19 us
    dot_general x10 -> x2, matrix products: 91.9 us -> 22.6 us  [the longest x1 11.9 us: on_device(): partial = jnp.dot(hidden, w_out_whole, preferred_element_type=jnp.float32)]
    all_gather x2 -> x0, blocking collectives: 22.6 us -> none  [the longest x1 11.8 us: on_device(): lax.all_gather(d_mixed_in, 'dp', axis=1, tiled=True)]
    pallas_call x0 -> x1, Pallas kernels: none -> 19 us  [attend(): pl.pallas_call(functools.partial(attend_kernel, rows=min(rows, 128)), gri...]
    all_gather x2 -> x0, local copies, waits for them, and re-layouts: 17.4 us -> none  [the longest x1 8.7 us: on_device(): lax.all_gather(d_value, 'seq', axis=0, tiled=True)]
    unnamed x26 -> x2, local copies, waits for them, and re-layouts: 10.2 us -> 0.01 us
    all_gather x6 -> x4, waiting for transfers between devices: 362 us -> 357 us  [the longest x1 129 us: on_device(): lax.all_gather(jnp.concatenate([key, value, d_key, d_value], axis=1), 'se...]
    reduce_scatter x2 -> x1, waiting for transfers between devices: 23.9 us -> 26.3 us  [on_device(): lax.psum_scatter(partial.astype(jnp.bfloat16), 'dp', scatter_dimension=1,...]
  transfers between devices with their start and end apart: 8 -> 5, of which waited for: 8 -> 5; matrix products, arithmetic and copies ran while one was open for 20% -> 3% of each run, Pallas kernels for 0% -> 4%
where the time goes in v1:
time: 448 us; the launch traced here: 446 us
  waiting for transfers between devices  384 us (86%)
  matrix products  22.6 us (5%)
  Pallas kernels  19 us (4%)
  between operations  13.8 us (3%)
  other arithmetic  5.24 us (1%)
    all_gather x1, waiting for transfers between devices, on_device(): lax.all_gather(jnp.concatenate([key, value, d_key, d_value], axis=1), 'se...  129 us
    all_gather x1, waiting for transfers between devices, on_device(): w_out_whole = lax.all_gather(w_out, 'seq', axis=0, tiled=True)  103 us
    all_gather x1, waiting for transfers between devices, on_device(): w_in_whole = lax.all_gather(w_in, 'seq', axis=0, tiled=True)  95.7 us
    all_gather x1, waiting for transfers between devices, on_device(): whole = lax.all_gather(mixed, 'dp', axis=1, tiled=True)  28.8 us
    reduce_scatter x1, waiting for transfers between devices, on_device(): lax.psum_scatter(partial.astype(jnp.bfloat16), 'dp', scatter_dimension=1,...  26.3 us
    pallas_call x1, Pallas kernels, attend(): pl.pallas_call(functools.partial(attend_kernel, rows=min(rows, 128)), gri...  19 us
    dot_general x1, matrix products, on_device(): partial = jnp.dot(hidden, w_out_whole, preferred_element_type=jnp.float32)  11.9 us
    dot_general x1, matrix products, on_device(): pre = jnp.dot(whole, w_in_whole, preferred_element_type=jnp.float32)  10.7 us
  transfers between devices with their start and end apart: 5, of which 5 were waited for; matrix products, arithmetic and copies ran while one was open for 3% of the time, Pallas kernels for 4%

profile of v1, /device:TPU:8, one launch (start us, length us, event | category | flops | bytes accessed | tf_op | source)
XLA Modules:
  0.0 446.1 jit_solution(11088575822397013597)
XLA Ops:
  7.2 0.0 all-gather.5.cloned.1.call-start
  7.2 2.7 pad_maximum_fusion
  9.9 0.0 all-gather.5.cloned.1.call-update
  9.9 0.0 all-gather.9.cloned.1.call-start
  10.0 0.7 all-gather.9.cloned.1.call-update
  10.7 0.0 all-gather.7.cloned.1.call-start
  10.7 129.0 %all-gather.5.cloned.1.call-done.k.v.dk.dv = bf16[2048,6144]{1,0:T(8,128)(2,1)} async-done(((bf16[128,6144]{1,0:T(8,128)(2,1)}), bf16[2048,6144]{1,0:T(8,128)(2,1)}) %all-gather.5.cloned.1.call-update) | async-done | bytes 25165840 | tf_op jit(solution)/shard_map/all_gather | solution.py:83
  139.7 19.0 %attend.1 = bf16[2,128,1536]{2,1,0:T(8,128)(2,1)} custom-call(bf16[128,1536]{1,0:T(8,128)(2,1)} %q.1, bf16[128,1536]{1,0:T(8,128)(2,1)} %dq.1, bf16[128,1536]{1,0:T(8,128)(2,1)} %res.1, bf16[128,1536]{1,0:T(8,128)(2,1)} %dres.1, bf16[2048,6144]{1,0:T(8,128)(2,1)} %all-gather.5.cloned.1.call-done.k.v.dk.dv, ...), custom_call_target="tpu_custom_call" | custom-call | flops 4831838208 | bytes 25165824 | tf_op jit(solution)/shard_map/attend/pallas_call | solution.py:68
  158.7 0.0 all-gather.7.cloned.1.call-update
  158.7 0.0 all-gather.11.cloned.1.call-start
  158.8 0.5 all-gather.11.cloned.1.call-update
  159.3 0.0 reduce-scatter.2.cloned.1.call-start
  159.4 95.7 %all-gather.9.cloned.1.call-done = bf16[3072,3584]{1,0:T(8,128)(2,1)} async-done(((bf16[192,3584]{1,0:T(8,128)(2,1)}), bf16[3072,3584]{1,0:T(8,128)(2,1)}) %all-gather.9.cloned.1.call-update) | async-done | bytes 22020112 | tf_op jit(solution)/shard_map/all_gather | solution.py:86
  255.1 28.8 %all-gather.7.cloned.1.call-done = bf16[256,3072]{1,0:T(8,128)(2,1)} async-done(((bf16[256,1536]{1,0:T(8,128)(2,1)}), bf16[256,3072]{1,0:T(8,128)(2,1)}) %all-gather.7.cloned.1.call-update) | async-done | bytes 1572880 | tf_op jit(solution)/shard_map/all_gather | solution.py:89
  283.9 10.7 %fusion.12 = f32[256,3584]{1,0:T(8,128)S(1)} fusion(bf16[256,3072]{1,0:T(8,128)(2,1)} %all-gather.7.cloned.1.call-done, bf16[3072,3584]{1,0:T(8,128)(2,1)} %all-gather.9.cloned.1.call-done), kind=kOutput, calls=%fused_computation.18 | convolution fusion | flops 5637144576 | bytes 27262976 | tf_op jit(solution)/shard_map/dot_general | solution.py:90
  294.6 1.2 multiply_convert_fusion
  295.9 103.2 %all-gather.11.cloned.1.call-done = bf16[3584,3072]{1,0:T(8,128)(2,1)} async-done(((bf16[224,3072]{1,0:T(8,128)(2,1)}), bf16[3584,3072]{1,0:T(8,128)(2,1)}) %all-gather.11.cloned.1.call-update) | async-done | bytes 22020112 | tf_op jit(solution)/shard_map/all_gather | solution.py:87
  399.1 11.9 %convolution_convert_fusion = bf16[256,3072]{1,0:T(8,128)(2,1)} fusion(bf16[3584,3072]{1,0:T(8,128)(2,1)} %all-gather.11.cloned.1.call-done, bf16[128,3584]{1,0:T(8,128)(2,1)S(1)} %get-tuple-element.3, bf16[128,3584]{1,0:T(8,128)(2,1)S(1)} %get-tuple-element.2), kind=kOutput, calls=%fused_computation | convolution fusion | flops 5641601024 | bytes 25427968 | tf_op jit(solution)/shard_map/dot_general | solution.py:93
  411.0 0.0 copy-start
  411.0 0.0 reduce-scatter.2.cloned.1.call-update
  411.0 26.3 %reduce-scatter.2.cloned.1.call-done = bf16[256,1536]{1,0:T(8,128)(2,1)} async-done(((bf16[256,3072]{1,0:T(8,128)(2,1)}), bf16[256,1536]{1,0:T(8,128)(2,1)}) %reduce-scatter.2.cloned.1.call-update) | async-done | bytes 786448 | tf_op jit(solution)/shard_map/reduce_scatter | solution.py:94
  437.3 0.0 copy-done
  437.3 1.3 add_convert_fusion
  438.6 0.9 fusion.11
Async XLA Ops:
  7.2 132.6 %all-gather.5.cloned.1.call-start = ((), (), s32[]{:S(2)}) async-start(), calls=%async_computation.1 | async-start | bytes 26738688 | tf_op jit(solution)/shard_map/all_gather | solution.py:83
  9.9 245.2 %all-gather.9.cloned.1.call-start = ((), (), s32[]{:S(2)}) async-start(), calls=%async_computation.3 | async-start | bytes 23396352 | tf_op jit(solution)/shard_map/all_gather | solution.py:86
  10.7 273.2 %all-gather.7.cloned.1.call-start = ((), (), s32[]{:S(2)}) async-start(), calls=%async_computation.2 | async-start | bytes 2359296 | tf_op jit(solution)/shard_map/all_gather | solution.py:89
  158.7 240.3 %all-gather.11.cloned.1.call-start = ((), (), s32[]{:S(2)}) async-start(), calls=%async_computation.4 | async-start | bytes 23396352 | tf_op jit(solution)/shard_map/all_gather | solution.py:87
  159.3 278.0 %reduce-scatter.2.cloned.1.call-start = ((), (), s32[]{:S(2)}) async-start(), calls=%async_computation.5 | async-start | bytes 2359296 | tf_op jit(solution)/shard_map/reduce_scatter | solution.py:94
  411.0 26.3 %copy-start = (bf16[2,128,1536]{2,1,0:T(8,128)(2,1)S(1)}, bf16[2,128,1536]{2,1,0:T(8,128)(2,1)}, u32[]{:S(2)}) copy-start(bf16[2,128,1536]{2,1,0:T(8,128)(2,1)} %attend.1) | copy-start | bytes 2359300
Sparse Core Ops, SparseCore 0:
  10.0 129.6 all-gather.4
  141.3 113.6 all-gather.8
  256.6 27.2 all-gather.6
  285.3 113.7 all-gather.10
  411.1 26.1 reduce-scatter.1

commit v2 on v1

--- a/solution.py
+++ b/solution.py
@@ -29,31 +29,37 @@
     return lax.dot_general(a, b, (((1,), (1,)), ((), ())), preferred_element_type=jnp.float32)
 
 
+def attend_math(q, dq, res, dres, keys, values, keys_pair, values_pair):
+    scale = 1.0 / math.sqrt(HEAD_DIM)
+    scores = nt(q, keys) * scale
+    d_scores = nt(jnp.concatenate([dq, q], axis=1), keys_pair) * scale
+    peak = jnp.max(scores, axis=1, keepdims=True)
+    weights = jnp.exp(scores - peak)
+    mixed = weights * d_scores
+    total = jnp.sum(weights, axis=1, keepdims=True)
+    slope = jnp.sum(mixed, axis=1, keepdims=True)
+    both = jnp.dot(weights.astype(jnp.bfloat16), values_pair, preferred_element_type=jnp.float32)
+    tangent = both[:, HEAD_DIM:] + jnp.dot(
+        mixed.astype(jnp.bfloat16), values, preferred_element_type=jnp.float32
+    )
+    attended = both[:, :HEAD_DIM] / total
+    d_attended = tangent / total - (slope / total) * attended
+    return (
+        (res.astype(jnp.float32) + attended).astype(jnp.bfloat16),
+        (dres.astype(jnp.float32) + d_attended).astype(jnp.bfloat16),
+    )
+
+
 def attend_kernel(q, dq, res, dres, k, v, dk, dv, out, *, rows):
-    scale = 1.0 / math.sqrt(HEAD_DIM)
-    keys = k[...]
+    keys, values = k[...], v[...]
     keys_pair = jnp.concatenate([keys, dk[...]], axis=1)
-    values = v[...]
     values_pair = jnp.concatenate([values, dv[...]], axis=1)
     for start in range(0, q.shape[0], rows):
         part = pl.ds(start, rows)
-        scores = nt(q[part, :], keys) * scale
-        d_scores = nt(jnp.concatenate([dq[part, :], q[part, :]], axis=1), keys_pair) * scale
-        peak = jnp.max(scores, axis=1, keepdims=True)
-        weights = jnp.exp(scores - peak)
-        mixed = weights * d_scores
-        total = jnp.sum(weights, axis=1, keepdims=True)
-        slope = jnp.sum(mixed, axis=1, keepdims=True)
-        both = jnp.dot(
-            weights.astype(jnp.bfloat16), values_pair, preferred_element_type=jnp.float32
-        )
-        tangent = both[:, HEAD_DIM:] + jnp.dot(
-            mixed.astype(jnp.bfloat16), values, preferred_element_type=jnp.float32
-        )
-        attended = both[:, :HEAD_DIM] / total
-        d_attended = tangent / total - (slope / total) * attended
-        out[0, part, :] = (res[part, :].astype(jnp.float32) + attended).astype(jnp.bfloat16)
-        out[1, part, :] = (dres[part, :].astype(jnp.float32) + d_attended).astype(jnp.bfloat16)
+        out[0, part, :], out[1, part, :] = attend_math(
+            q[part, :], dq[part, :], res[part, :], dres[part, :],
+            keys, values, keys_pair, values_pair,
+        )
 
 
 def attend(query, d_query, residual, d_residual, kv):
@@ -78,7 +84,7 @@
     )(query, d_query, residual, d_residual, kv, kv, kv, kv)
 
 
-def on_device(query, key, value, d_query, d_key, d_value, residual, d_residual, w_in, w_out):
+def by_rows(query, key, value, d_query, d_key, d_value, residual, d_residual, w_in, w_out):
     rows, feats = query.shape
     kv = lax.all_gather(
         jnp.concatenate([key, value, d_key, d_value], axis=1), "seq", axis=0, tiled=True
@@ -98,9 +104,384 @@
     return (out[:rows], out[rows:])
 
 
+INNER = 4
+MESH = pl.DeviceIdType.MESH
+
+
+def place(groups):
+    seq = lax.axis_index("seq")
+    return lax.axis_index("dp"), lax.div(seq, INNER), lax.rem(seq, INNER)
+
+
+def enter(devices):
+    barrier = pltpu.get_barrier_semaphore()
+    for device in devices:
+        pl.semaphore_signal(barrier, inc=1, device_id=device, device_id_type=MESH)
+    pl.semaphore_wait(barrier, len(devices))
+
+
+def spread_kernel(
+    q, dq, res, dres, k, v, dk, dv, w_in, own, kv, win, z_send, z_recv, own_sem,
+    p_send, p_recv, y_send, y_recv, f_send, f_recv,
+):
+    groups, width = own.shape[1], own.shape[3]
+    hid = win.shape[2]
+    x, g, i = place(groups)
+    partner = (x, g * INNER + i + 1 - 2 * lax.rem(i, 2))
+    across_i = lax.rem(i + 2, INNER)
+    across = (x, g * INNER + across_i)
+    peers = [(x, lax.rem(g + t, groups) * INNER + i) for t in range(1, groups)]
+    enter(peers + [partner, across])
+
+    def piece(j, to):
+        if j < 4:
+            return (k, v, dk, dv)[j].at[:, pl.ds(pl.multiple_of(to * width, 128), width)]
+        if j < 8:
+            return (q, dq, res, dres)[j - 4].at[:, pl.ds(pl.multiple_of(to * width, 128), width)]
+        return w_in.at[:, pl.ds(pl.multiple_of(to * hid, 128), hid)]
+
+    def slot(j, source):
+        if j < 4:
+            return kv.at[i, source, j]
+        if j < 8:
+            return own.at[j - 4, source]
+        return win.at[source]
+
+    def over_z(t, j):
+        return pltpu.make_async_remote_copy(
+            src_ref=piece(j, lax.rem(g + t, groups)),
+            dst_ref=slot(j, g),
+            send_sem=z_send.at[t - 1, j],
+            recv_sem=z_recv.at[t - 1, j],
+            device_id=peers[t - 1],
+            device_id_type=MESH,
+        )
+
+    def layer(block, source, send, recv, t, device):
+        return pltpu.make_async_remote_copy(
+            src_ref=kv.at[block, source],
+            dst_ref=kv.at[block, source],
+            send_sem=send.at[t],
+            recv_sem=recv.at[t],
+            device_id=device,
+            device_id_type=MESH,
+        )
+
+    z_copies = {}
+    for order in (range(8), (8,)):
+        for t in range(1, groups):
+            for j in order:
+                z_copies[t, j] = over_z(t, j)
+                z_copies[t, j].start()
+    locals_ = [pltpu.make_async_copy(piece(j, g), slot(j, g), own_sem.at[j]) for j in range(9)]
+    for copy in locals_:
+        copy.start()
+    for copy in locals_:
+        copy.wait()
+    inside, forwards = [], []
+
+    def forward(t):
+        inside[t][1].wait_recv()
+        source = lax.rem(g + groups - t, groups)
+        copy = layer(across_i, source, f_send, f_recv, t, partner)
+        copy.start()
+        forwards.append(copy)
+
+    for t in range(groups):
+        if t:
+            for j in range(4):
+                z_copies[t, j].wait_recv()
+        source = lax.rem(g + groups - t, groups)
+        pair = (
+            layer(i, source, p_send, p_recv, t, partner),
+            layer(i, source, y_send, y_recv, t, across),
+        )
+        pair[1].start()
+        pair[0].start()
+        inside.append(pair)
+        if t:
+            forward(t - 1)
+    forward(groups - 1)
+    for t in range(groups):
+        inside[t][0].wait()
+        inside[t][1].wait_send()
+        forwards[t].wait()
+    for (t, j), copy in z_copies.items():
+        copy.wait_send()
+        if j >= 4:
+            copy.wait_recv()
+
+
+def spread(tensors, w_in, groups):
+    rows, feats = tensors[0].shape
+    width = feats // groups
+    deep, hid = w_in.shape[0], w_in.shape[1] // groups
+    dma = pltpu.SemaphoreType.DMA
+    return pl.pallas_call(
+        spread_kernel,
+        in_specs=[pl.BlockSpec(memory_space=pltpu.VMEM)] * 9,
+        out_specs=[pl.BlockSpec(memory_space=pl.ANY)] * 3,
+        out_shape=[
+            jax.ShapeDtypeStruct((4, groups, rows, width), jnp.bfloat16),
+            jax.ShapeDtypeStruct((INNER, groups, 4, rows, width), jnp.bfloat16),
+            jax.ShapeDtypeStruct((groups, deep, hid), jnp.bfloat16),
+        ],
+        scratch_shapes=[dma((groups - 1, 9)), dma((groups - 1, 9)), dma((9,))]
+        + [dma((groups,)) for _ in range(6)],
+        compiler_params=pltpu.CompilerParams(collective_id=0, has_side_effects=True),
+        name="spread",
+    )(*tensors, w_in)
+
+
+def attend_wide_kernel(q, dq, res, dres, k, v, dk, dv, out):
+    length = k.shape[0] * k.shape[1] * k.shape[3]
+    keys, values, d_keys, d_values = (
+        ref[...].reshape(length, HEAD_DIM) for ref in (k, v, dk, dv)
+    )
+    keys_pair = jnp.concatenate([keys, d_keys], axis=1)
+    values_pair = jnp.concatenate([values, d_values], axis=1)
+    half = out.shape[3]
+    for g in range(q.shape[1]):
+        pair = attend_math(
+            q[0, g], dq[0, g], res[0, g], dres[0, g], keys, values, keys_pair, values_pair
+        )
+        for side in range(out.shape[0]):
+            for kind in range(2):
+                out[side, kind, g] = pair[kind][side * half : (side + 1) * half]
+
+
+def attend_wide(own, kv, sides):
+    _, groups, rows, width = own.shape
+    heads = width // HEAD_DIM
+    half = rows // sides
+
+    def own_spec(i):
+        return pl.BlockSpec((1, groups, rows, HEAD_DIM), lambda h: (i, 0, 0, h))
+
+    def kv_spec(i):
+        return pl.BlockSpec((INNER, groups, 1, rows, HEAD_DIM), lambda h: (0, 0, i, 0, h))
+
+    return pl.pallas_call(
+        attend_wide_kernel,
+        grid=(heads,),
+        in_specs=[own_spec(i) for i in range(4)] + [kv_spec(i) for i in range(4)],
+        out_specs=pl.BlockSpec((sides, 2, groups, half, HEAD_DIM), lambda h: (0, 0, 0, 0, h)),
+        out_shape=jax.ShapeDtypeStruct((sides, 2, groups, half, width), jnp.bfloat16),
+        cost_estimate=pl.CostEstimate(
+            flops=12 * INNER * (groups * rows) ** 2 * width,
+            bytes_accessed=8 * INNER * groups * rows * width,
+            transcendentals=0,
+        ),
+        name="attend_wide",
+    )(own, own, own, own, kv, kv, kv, kv)
+
+
+def line_kernel(block, out, own_sem, right_send, right_recv, left_send, left_recv):
+    groups = out.shape[0]
+    x, g, i = place(groups)
+    last = groups - 1
+    right = (x, jnp.minimum(g + 1, last) * INNER + i)
+    left = (x, jnp.maximum(g - 1, 0) * INNER + i)
+    enter([(x, lax.rem(g + t, groups) * INNER + i) for t in range(1, groups)])
+
+    def hop(t, first, to_right):
+        source = g - t if to_right else g + t
+        sends, recvs = (right_send, right_recv) if to_right else (left_send, left_recv)
+        return pltpu.make_async_remote_copy(
+            src_ref=block if first else out.at[source],
+            dst_ref=out.at[source],
+            send_sem=sends.at[t],
+            recv_sem=recvs.at[t],
+            device_id=right if to_right else left,
+            device_id_type=MESH,
+        )
+
+    mine = pltpu.make_async_copy(block, out.at[g], own_sem)
+    mine.start()
+    for t in range(last):
+        if t:
+
+            @pl.when(g >= t)
+            def _():
+                hop(t - 1, False, True).wait_recv()
+
+        @pl.when((g >= t) & (g < last))
+        def _():
+            hop(t, t == 0, True).start()
+
+        if t:
+
+            @pl.when(g + t <= last)
+            def _():
+                hop(t - 1, False, False).wait_recv()
+
+        @pl.when((g + t <= last) & (g > 0))
+        def _():
+            hop(t, t == 0, False).start()
+
+    @pl.when(g >= last)
+    def _():
+        hop(last - 1, False, True).wait_recv()
+
+    @pl.when(g + last <= last)
+    def _():
+        hop(last - 1, False, False).wait_recv()
+
+    for t in range(last):
+
+        @pl.when((g >= t) & (g < last))
+        def _():
+            hop(t, t == 0, True).wait_send()
+
+        @pl.when((g + t <= last) & (g > 0))
+        def _():
+            hop(t, t == 0, False).wait_send()
+
+    mine.wait()
+
+
+def along_line(block, groups):
+    dma = pltpu.SemaphoreType.DMA
+    return pl.pallas_call(
+        line_kernel,
+        in_specs=[pl.BlockSpec(memory_space=pltpu.VMEM)],
+        out_specs=pl.BlockSpec(memory_space=pl.ANY),
+        out_shape=jax.ShapeDtypeStruct((groups,) + block.shape, block.dtype),
+        scratch_shapes=[dma] + [dma((groups - 1,)) for _ in range(4)],
+        compiler_params=pltpu.CompilerParams(collective_id=1, has_side_effects=True),
+        name="along_line",
+    )(block)
+
+
+def return_kernel(partial, out, own_sem, send, recv):
+    groups = out.shape[0]
+    x, g, i = place(groups)
+    peers = [(x, lax.rem(g + t, groups) * INNER + i) for t in range(1, groups)]
+    enter(peers)
+    copies = [
+        pltpu.make_async_remote_copy(
+            src_ref=partial.at[lax.rem(g + t, groups)],
+            dst_ref=out.at[t],
+            send_sem=send.at[t - 1],
+            recv_sem=recv.at[t - 1],
+            device_id=peers[t - 1],
+            device_id_type=MESH,
+        )
+        for t in range(1, groups)
+    ]
+    for copy in copies:
+        copy.start()
+    mine = pltpu.make_async_copy(partial.at[g], out.at[0], own_sem)
+    mine.start()
+    mine.wait()
+    for copy in copies:
+        copy.wait()
+
+
+def send_back(partial):
+    groups = partial.shape[0]
+    dma = pltpu.SemaphoreType.DMA
+    return pl.pallas_call(
+        return_kernel,
+        in_specs=[pl.BlockSpec(memory_space=pltpu.VMEM)],
+        out_specs=pl.BlockSpec(memory_space=pl.ANY),
+        out_shape=jax.ShapeDtypeStruct(partial.shape, partial.dtype),
+        scratch_shapes=[dma, dma((groups - 1,)), dma((groups - 1,))],
+        compiler_params=pltpu.CompilerParams(collective_id=2, has_side_effects=True),
+        name="send_back",
+    )(partial)
+
+
+def hidden_kernel(a, w, out, total):
+    step = pl.program_id(1)
+    left = jnp.concatenate([a[j, 0] for j in range(a.shape[0])], axis=1)
+    depth, hid = left.shape[1], w.shape[4]
+    product = jnp.dot(left, w[...].reshape(depth, hid), preferred_element_type=jnp.float32)
+
+    @pl.when(step == 0)
+    def _():
+        total[...] = product
+
+    @pl.when(step > 0)
+    def _():
+        total[...] += product
+
+    @pl.when(step == pl.num_programs(1) - 1)
+    def _():
+        rows = total.shape[0] // 2
+        value, tangent = gelu_pair(total[:rows], total[rows:])
+        out[:rows] = value.astype(jnp.bfloat16)
+        out[rows:] = tangent.astype(jnp.bfloat16)
+
+
+def hidden_layer(gathered, w, dp):
+    groups, _, rows, width = gathered.shape
+    deep, hid = w.shape[3:]
+    per = groups // dp
+    return pl.pallas_call(
+        hidden_kernel,
+        grid=(dp, groups),
+        in_specs=[
+            pl.BlockSpec((dp, 1, rows, width), lambda f, k: (lax.rem(k, per), lax.div(k, per), 0, 0)),
+            pl.BlockSpec((1, INNER, 1, deep, hid), lambda f, k: (f, 0, k, 0, 0)),
+        ],
+        out_specs=pl.BlockSpec((rows, hid), lambda f, k: (0, f)),
+        out_shape=jax.ShapeDtypeStruct((rows, dp * hid), jnp.bfloat16),
+        scratch_shapes=[pltpu.VMEM((rows, hid), jnp.float32)],
+        cost_estimate=pl.CostEstimate(
+            flops=2 * rows * groups * dp * width * dp * hid,
+            bytes_accessed=2 * dp * INNER * groups * deep * hid,
+            transcendentals=0,
+        ),
+        name="hidden_layer",
+    )(gathered, w)
+
+
+def in_layer(block, dp, seq):
+    layers = [
+        [d * seq + layer * INNER + i for d in range(dp) for i in range(INNER)]
+        for layer in range(seq // INNER)
+    ]
+    return lax.all_gather(block, ("dp", "seq"), axis_index_groups=layers, axis=0, tiled=False)
+
+
+def by_layers(query, key, value, d_query, d_key, d_value, residual, d_residual, w_in, w_out, dp, seq):
+    groups = seq // INNER
+    rows, feats = query.shape
+    half, width = rows // dp, feats // groups
+    w_out_layer = in_layer(w_out, dp, seq).reshape(dp * INNER * w_out.shape[0], w_out.shape[1])
+    own, kv, win = spread(
+        (query, d_query, residual, d_residual, key, value, d_key, d_value), w_in, groups
+    )
+    w_in_layer = in_layer(win, dp, seq).reshape((dp, INNER) + win.shape)
+    mixed = attend_wide(own, kv, dp)
+    block = lax.all_to_all(mixed, "dp", split_axis=0, concat_axis=0, tiled=True)
+    gathered = along_line(block, groups)
+    hidden = hidden_layer(gathered.reshape(groups, dp, 2 * groups * half, width), w_in_layer, dp)
+    partial = jnp.dot(hidden, w_out_layer, preferred_element_type=jnp.float32).astype(jnp.bfloat16)
+    partial = partial.reshape(2, groups, half, dp * feats).transpose(1, 0, 2, 3)
+    sums = jnp.sum(send_back(partial).astype(jnp.float32), axis=0)
+    g = lax.div(lax.axis_index("seq"), INNER)
+    base = lax.dynamic_index_in_dim(gathered, g, axis=3, keepdims=False)
+    base = base.transpose(2, 3, 1, 0, 4).reshape(2, half, dp * feats)
+    done = (base.astype(jnp.float32) + sums).astype(jnp.bfloat16)
+    out = lax.all_to_all(done, "dp", split_axis=2, concat_axis=1, tiled=True)
+    return (out[0], out[1])
+
+
+def on_device(*args, dp, seq):
+    query, w_in = args[0], args[8]
+    groups = seq // INNER
+    tile = groups * HEAD_DIM
+    if seq % INNER or groups < 2 or groups % dp or query.shape[1] % tile or w_in.shape[1] % tile:
+        return by_rows(*args)
+    return by_layers(*args, dp=dp, seq=seq)
+
+
 def solution(mesh):
     in_specs = (P("seq", "dp"),) * 9 + (P(("dp", "seq"), None),)
     out_specs = (P("seq", "dp"), P("seq", "dp"))
+    body = functools.partial(on_device, dp=mesh.shape["dp"], seq=mesh.shape["seq"])
     return jax.shard_map(
-        on_device, mesh=mesh, in_specs=in_specs, out_specs=out_specs, check_vma=False
-    )
+        body, mesh=mesh, in_specs=in_specs, out_specs=out_specs, check_vma=False
+    )

time: 448 us -> 367 us (0.82)
  waiting for transfers between devices: 384 us -> 48.9 us
  Pallas kernels: 19 us -> 261 us
  blocking collectives: 0 us -> 13.7 us
  matrix products: 22.6 us -> 9.24 us
  local copies, waits for them, and re-layouts: 0.93 us -> 12 us
    all_gather x4 -> x2, waiting for transfers between devices: 357 us -> 31.3 us  [in_layer(): lax.all_gather(block, ('dp', 'seq'), axis_index_groups=layers, axis=0, ti...]
    pallas_call x1 -> x5, Pallas kernels: 19 us -> 261 us  [the longest x1 104 us: spread(): pl.pallas_call(spread_kernel, in_specs=[pl.BlockSpec(memory_space=pltpu.V...]
    reduce_scatter x1 -> x0, waiting for transfers between devices: 26.3 us -> none  [on_device(): lax.psum_scatter(partial.astype(jnp.bfloat16), 'dp', scatter_dimension=1,...]
    all_to_all x0 -> x1, waiting for transfers between devices: none -> 16.9 us  [by_layers(): block = lax.all_to_all(mixed, 'dp', split_axis=0, concat_axis=0, tiled=True)]
    all_to_all x0 -> x1, blocking collectives: none -> 13.7 us  [by_layers(): out = lax.all_to_all(done, 'dp', split_axis=2, concat_axis=1, tiled=True)]
    dot_general x2 -> x1, matrix products: 22.6 us -> 9.24 us  [by_layers(): jnp.dot(hidden, w_out_layer, preferred_element_type=jnp.float32)]
  transfers between devices with their start and end apart: 5 -> 3, of which waited for: 5 -> 2; matrix products, arithmetic and copies ran while one was open for 3% -> 1% of each run, Pallas kernels for 4% -> 23%
where the time goes in v2:
time: 367 us
  Pallas kernels  261 us (71%)
  waiting for transfers between devices  48.9 us (13%)
  between operations  14.2 us (4%)
  blocking collectives  13.7 us (4%)
  local copies, waits for them, and re-layouts  12 us (3%)
  matrix products  9.24 us (3%)
  other arithmetic  4.16 us (1%)
    pallas_call x1, Pallas kernels, spread(): pl.pallas_call(spread_kernel, in_specs=[pl.BlockSpec(memory_space=pltpu.V...  104 us
    pallas_call x1, Pallas kernels, send_back(): pl.pallas_call(return_kernel, in_specs=[pl.BlockSpec(memory_space=pltpu.V...  73.3 us
    pallas_call x1, Pallas kernels, along_line(): pl.pallas_call(line_kernel, in_specs=[pl.BlockSpec(memory_space=pltpu.VME...  55.2 us
    all_gather x2, waiting for transfers between devices, in_layer(): lax.all_gather(block, ('dp', 'seq'), axis_index_groups=layers, axis=0, ti...  31.3 us
    all_to_all x1, waiting for transfers between devices, by_layers(): block = lax.all_to_all(mixed, 'dp', split_axis=0, concat_axis=0, tiled=True)  16.9 us
    pallas_call x1, Pallas kernels, hidden_layer(): pl.pallas_call(hidden_kernel, grid=(dp, groups), in_specs=[pl.BlockSpec((...  15 us
    pallas_call x1, Pallas kernels, attend_wide(): pl.pallas_call(attend_wide_kernel, grid=(heads,), in_specs=[own_spec(i) f...  13.8 us
    all_to_all x1, blocking collectives, by_layers(): out = lax.all_to_all(done, 'dp', split_axis=2, concat_axis=1, tiled=True)  13.7 us
  transfers between devices with their start and end apart: 3, of which 2 were waited for; matrix products, arithmetic and copies ran while one was open for 1% of the time, Pallas kernels for 23%

profile of v2, /device:TPU:8, one launch (start us, length us, event | category | flops | bytes accessed | tf_op | source)
XLA Modules:
  0.0 366.7 jit_solution(5468845842435545640)
XLA Ops:
  7.2 0.0 all-gather.5.cloned.1.call-start
  7.2 103.8 %spread.1 = (bf16[4,4,128,384]{3,2,1,0:T(8,128)(2,1)}, bf16[4,4,4,128,384]{4,3,2,1,0:T(8,128)(2,1)}, bf16[4,192,896]{2,1,0:T(8,128)(2,1)}) custom-call(bf16[128,1536]{1,0:T(8,128)(2,1)} %q.1, bf16[128,1536]{1,0:T(8,128)(2,1)} %dq.1, bf16[128,1536]{1,0:T(8,128)(2,1)} %res.1, bf16[128,1536]{1,0:T(8,128)(2,1)} %dres.1, bf16[128,1536]{1,0:T(8,128)(2,1)} %k.1, ...), custom_call_target="tpu_custom_call" | custom-call | tf_op jit(solution)/shard_map/spread/pallas_call | solution.py:220
  111.0 0.0 all-gather.5.cloned.1.call-update
  111.0 0.0 all-gather.7.cloned.1.call-start
  111.0 0.7 all-gather.7.cloned.1.call-update
  111.8 13.8 %attend_wide.1 = bf16[2,2,4,64,384]{4,3,2,1,0:T(8,128)(2,1)} custom-call(bf16[4,4,128,384]{3,2,1,0:T(8,128)(2,1)} %get-tuple-element.5.q.dq.res.dres, bf16[4,4,128,384]{3,2,1,0:T(8,128)(2,1)} %get-tuple-element.5.q.dq.res.dres, bf16[4,4,128,384]{3,2,1,0:T(8,128)(2,1)} %get-tuple-element.5.q.dq.res.dres, ...), custom_call_target="tpu_custom_call" | custom-call | flops 4831838208 | bytes 6291456 | tf_op jit(solution)/shard_map/attend_wide/pallas_call | solution.py:264
  125.5 3.5 all-to-all-start
  129.1 16.9 %all-to-all-done.block = bf16[2,2,4,64,384]{4,3,2,1,0:T(8,128)(2,1)S(1)} async-done(((bf16[2,2,4,64,384]{4,3,2,1,0:T(8,128)(2,1)}), bf16[2,2,4,64,384]{4,3,2,1,0:T(8,128)(2,1)S(1)}, u32[]{:S(2)}, u32[]{:S(2)}) %all-to-all-start) | async-done | bytes 786464 | tf_op jit(solution)/shard_map/all_to_all | solution.py:458
  146.0 0.0 copy-start
  146.0 0.9 copy-done
  147.0 55.2 %along_line.1 = bf16[4,2,2,4,64,384]{5,4,3,2,1,0:T(8,128)(2,1)} custom-call(bf16[2,2,4,64,384]{4,3,2,1,0:T(8,128)(2,1)} %copy-done), custom_call_target="tpu_custom_call" | custom-call | tf_op jit(solution)/shard_map/along_line/pallas_call | solution.py:345
  202.1 1.3 convert_bitcast_fusion
  203.5 1.0 copy.18
  204.5 0.6 reshape.29
  205.1 0.0 all-gather.5.cloned.1.call-done
  205.1 15.0 %hidden_layer.1 = bf16[512,1792]{1,0:T(8,128)(2,1)} custom-call(bf16[4,2,512,384]{3,2,1,0:T(8,128)(2,1)} %bitcast.22, bf16[2,4,4,192,896]{4,3,2,1,0:T(8,128)(2,1)} %bitcast.27), custom_call_target="tpu_custom_call" | custom-call | flops 5637144576 | bytes 11010048 | tf_op jit(solution)/shard_map/hidden_layer/pallas_call | solution.py:421
  220.1 31.3 %all-gather.7.cloned.1.call-done = bf16[1792,3072]{1,0:T(8,128)(2,1)} async-done(((bf16[224,3072]{1,0:T(8,128)(2,1)}), bf16[1792,3072]{1,0:T(8,128)(2,1)}) %all-gather.7.cloned.1.call-update) | async-done | bytes 11010064 | tf_op jit(solution)/shard_map/all_gather | solution.py:445
  251.4 9.2 %convolution_convert_fusion = bf16[512,3072]{1,0:T(8,128)(2,1)S(1)} fusion(bf16[512,1792]{1,0:T(8,128)(2,1)} %hidden_layer.1, bf16[1792,3072]{1,0:T(8,128)(2,1)} %all-gather.7.cloned.1.call-done), kind=kOutput, calls=%fused_computation.1 | convolution fusion | flops 5638717440 | bytes 15990784 | tf_op jit(solution)/shard_map/dot_general | solution.py:461
  260.6 1.8 copy.26
  262.4 73.3 %send_back.1 = bf16[4,2,64,3072]{3,2,1,0:T(8,128)(2,1)} custom-call(bf16[4,2,64,3072]{3,2,1,0:T(8,128)(2,1)} %bitcast.19), custom_call_target="tpu_custom_call" | custom-call | tf_op jit(solution)/shard_map/send_back/pallas_call | solution.py:384
  335.7 2.6 convert_reduce_fusion
  338.4 0.2 add_convert_fusion
  338.6 1.9 copy.20
  340.5 1.2 reshape.35
  341.7 13.7 %all_to_all.20 = bf16[2,2,98304]{2,1,0:T(2,128)(2,1)S(1)} all-to-all(bf16[2,2,98304]{2,1,0:T(2,128)(2,1)S(1)} %reshape.35), channel_id=1, replica_groups=mesh['dp'=2,'seq'=16] {'dp'}, dimensions={0} | all-to-all | bytes 1572864 | tf_op jit(solution)/shard_map/all_to_all | solution.py:468
  355.4 1.0 reshape.36
  356.5 1.3 copy.24
  357.8 0.5 fusion
  358.3 0.8 copy.22
  359.1 0.8 copy.23
Async XLA Ops:
  7.2 198.0 %all-gather.5.cloned.1.call-start = ((), (), s32[]{:S(2)}) async-start(), calls=%async_computation.2 | async-start | bytes 12386304 | tf_op jit(solution)/shard_map/all_gather | solution.py:445
  111.0 140.4 %all-gather.7.cloned.1.call-start = ((), (), s32[]{:S(2)}) async-start(), calls=%async_computation.3 | async-start | bytes 12386304 | tf_op jit(solution)/shard_map/all_gather | solution.py:445
  125.5 20.5 %all-to-all-start = ((bf16[2,2,4,64,384]{4,3,2,1,0:T(8,128)(2,1)}), bf16[2,2,4,64,384]{4,3,2,1,0:T(8,128)(2,1)S(1)}, u32[]{:S(2)}, u32[]{:S(2)}) async-start(bf16[2,2,4,64,384]{4,3,2,1,0:T(8,128)(2,1)} %attend_wide.1), calls=%async_computation | async-start | bytes 1572864 | tf_op jit(solution)/shard_map/all_to_all | solution.py:458
  146.0 1.0 copy-start
Sparse Core Ops, SparseCore 0:
  111.1 72.9 all-gather.4
  186.0 65.3 all-gather.6

commit v3 on v2

--- a/solution.py
+++ b/solution.py
@@ -106,6 +106,7 @@
 
 INNER = 4
 MESH = pl.DeviceIdType.MESH
+COMM_COST = pl.CostEstimate(flops=10**11, bytes_accessed=10**8, transcendentals=0)
 
 
 def place(groups):
@@ -228,6 +229,7 @@
         ],
         scratch_shapes=[dma((groups - 1, 9)), dma((groups - 1, 9)), dma((9,))]
         + [dma((groups,)) for _ in range(6)],
+        cost_estimate=COMM_COST,
         compiler_params=pltpu.CompilerParams(collective_id=0, has_side_effects=True),
         name="spread",
     )(*tensors, w_in)
@@ -276,120 +278,182 @@
     )(own, own, own, own, kv, kv, kv, kv)
 
 
-def line_kernel(block, out, own_sem, right_send, right_recv, left_send, left_recv):
+def line_kernel(
+    mixed, out, own_sem, x_send, x_recv, right_send, right_recv, left_send, left_recv
+):
     groups = out.shape[0]
     x, g, i = place(groups)
     last = groups - 1
+    other = 1 - x
     right = (x, jnp.minimum(g + 1, last) * INNER + i)
     left = (x, jnp.maximum(g - 1, 0) * INNER + i)
-    enter([(x, lax.rem(g + t, groups) * INNER + i) for t in range(1, groups)])
-
-    def hop(t, first, to_right):
+    twin = (other, g * INNER + i)
+    enter([(x, lax.rem(g + t, groups) * INNER + i) for t in range(1, groups)] + [twin])
+
+    def hop(c, t, to_right):
         source = g - t if to_right else g + t
         sends, recvs = (right_send, right_recv) if to_right else (left_send, left_recv)
+        side = other if c else x
         return pltpu.make_async_remote_copy(
-            src_ref=block if first else out.at[source],
-            dst_ref=out.at[source],
-            send_sem=sends.at[t],
-            recv_sem=recvs.at[t],
+            src_ref=mixed.at[x] if c == 0 and t == 0 else out.at[source, side],
+            dst_ref=out.at[source, side],
+            send_sem=sends.at[c, t],
+            recv_sem=recvs.at[c, t],
             device_id=right if to_right else left,
             device_id_type=MESH,
         )
 
-    mine = pltpu.make_async_copy(block, out.at[g], own_sem)
+    swap = pltpu.make_async_remote_copy(
+        src_ref=mixed.at[other],
+        dst_ref=out.at[g, x],
+        send_sem=x_send,
+        recv_sem=x_recv,
+        device_id=twin,
+        device_id_type=MESH,
+    )
+    swap.start()
+    mine = pltpu.make_async_copy(mixed.at[x], out.at[g, x], own_sem)
     mine.start()
+
+    def sends_right(t):
+        return (g >= t) & (g < last)
+
+    def sends_left(t):
+        return (g + t <= last) & (g > 0)
+
     for t in range(last):
-        if t:
-
-            @pl.when(g >= t)
+        for c in range(2):
+            if t == 0 and c:
+                swap.wait_recv()
+            if t:
+
+                @pl.when(g >= t)
+                def _():
+                    hop(c, t - 1, True).wait_recv()
+
+            @pl.when(sends_right(t))
             def _():
-                hop(t - 1, False, True).wait_recv()
-
-        @pl.when((g >= t) & (g < last))
+                hop(c, t, True).start()
+
+            if t:
+
+                @pl.when(g + t <= last)
+                def _():
+                    hop(c, t - 1, False).wait_recv()
+
+            @pl.when(sends_left(t))
+            def _():
+                hop(c, t, False).start()
+
+    for c in range(2):
+
+        @pl.when(g >= last)
         def _():
-            hop(t, t == 0, True).start()
-
-        if t:
-
-            @pl.when(g + t <= last)
+            hop(c, last - 1, True).wait_recv()
+
+        @pl.when(g <= 0)
+        def _():
+            hop(c, last - 1, False).wait_recv()
+
+        for t in range(last):
+
+            @pl.when(sends_right(t))
             def _():
-                hop(t - 1, False, False).wait_recv()
-
-        @pl.when((g + t <= last) & (g > 0))
-        def _():
-            hop(t, t == 0, False).start()
-
-    @pl.when(g >= last)
-    def _():
-        hop(last - 1, False, True).wait_recv()
-
-    @pl.when(g + last <= last)
-    def _():
-        hop(last - 1, False, False).wait_recv()
-
-    for t in range(last):
-
-        @pl.when((g >= t) & (g < last))
-        def _():
-            hop(t, t == 0, True).wait_send()
-
-        @pl.when((g + t <= last) & (g > 0))
-        def _():
-            hop(t, t == 0, False).wait_send()
-
+                hop(c, t, True).wait_send()
+
+            @pl.when(sends_left(t))
+            def _():
+                hop(c, t, False).wait_send()
+
+    swap.wait_send()
     mine.wait()
 
 
-def along_line(block, groups):
+def along_line(mixed, groups):
     dma = pltpu.SemaphoreType.DMA
     return pl.pallas_call(
         line_kernel,
         in_specs=[pl.BlockSpec(memory_space=pltpu.VMEM)],
         out_specs=pl.BlockSpec(memory_space=pl.ANY),
-        out_shape=jax.ShapeDtypeStruct((groups,) + block.shape, block.dtype),
-        scratch_shapes=[dma] + [dma((groups - 1,)) for _ in range(4)],
+        out_shape=jax.ShapeDtypeStruct((groups,) + mixed.shape, mixed.dtype),
+        scratch_shapes=[dma] * 3 + [dma((2, groups - 1)) for _ in range(4)],
+        cost_estimate=COMM_COST,
         compiler_params=pltpu.CompilerParams(collective_id=1, has_side_effects=True),
         name="along_line",
-    )(block)
-
-
-def return_kernel(partial, out, own_sem, send, recv):
-    groups = out.shape[0]
+    )(mixed)
+
+
+def return_kernel(partial, gathered, out, base, own_sem, send, recv, base_send, base_recv):
+    groups, feats = out.shape[1], out.shape[4]
     x, g, i = place(groups)
-    peers = [(x, lax.rem(g + t, groups) * INNER + i) for t in range(1, groups)]
-    enter(peers)
+    steps = [(d, t) for t in range(groups) for d in range(2) if d or t]
+    sides = (x, 1 - x)
+    rows = [lax.rem(g + t, groups) for t in range(groups)]
+    enter([(sides[d], rows[t] * INNER + i) for d, t in steps])
+
+    def piece(d, t):
+        return partial.at[:, rows[t], :, pl.ds(pl.multiple_of(sides[d] * feats, 128), feats)]
+
     copies = [
         pltpu.make_async_remote_copy(
-            src_ref=partial.at[lax.rem(g + t, groups)],
-            dst_ref=out.at[t],
-            send_sem=send.at[t - 1],
-            recv_sem=recv.at[t - 1],
-            device_id=peers[t - 1],
+            src_ref=piece(d, t),
+            dst_ref=out.at[x, t],
+            send_sem=send.at[d, t],
+            recv_sem=recv.at[d, t],
+            device_id=(sides[d], rows[t] * INNER + i),
             device_id_type=MESH,
         )
-        for t in range(1, groups)
+        for d, t in sorted(steps, reverse=True)
     ]
+    for k in range(groups):
+        copies.append(
+            pltpu.make_async_remote_copy(
+                src_ref=gathered.at[k, sides[1], :, g],
+                dst_ref=base.at[k],
+                send_sem=base_send.at[k],
+                recv_sem=base_recv.at[k],
+                device_id=(sides[1], g * INNER + i),
+                device_id_type=MESH,
+            )
+        )
     for copy in copies:
         copy.start()
-    mine = pltpu.make_async_copy(partial.at[g], out.at[0], own_sem)
+    mine = pltpu.make_async_copy(piece(0, 0), out.at[x, 0], own_sem)
     mine.start()
     mine.wait()
     for copy in copies:
-        copy.wait()
-
-
-def send_back(partial):
-    groups = partial.shape[0]
+        copy.wait_send()
+    for d, t in steps:
+        pltpu.make_async_remote_copy(
+            src_ref=piece(d, t),
+            dst_ref=out.at[sides[d], t],
+            send_sem=send.at[d, t],
+            recv_sem=recv.at[d, t],
+            device_id=(sides[d], rows[t] * INNER + i),
+            device_id_type=MESH,
+        ).wait_recv()
+    for copy in copies[len(steps) :]:
+        copy.wait_recv()
+
+
+def send_back(partial, gathered):
+    groups, dp = gathered.shape[:2]
+    kinds, _, half, width = gathered.shape[2:]
+    feats = partial.shape[3] // dp
     dma = pltpu.SemaphoreType.DMA
     return pl.pallas_call(
         return_kernel,
-        in_specs=[pl.BlockSpec(memory_space=pltpu.VMEM)],
-        out_specs=pl.BlockSpec(memory_space=pl.ANY),
-        out_shape=jax.ShapeDtypeStruct(partial.shape, partial.dtype),
-        scratch_shapes=[dma, dma((groups - 1,)), dma((groups - 1,))],
+        in_specs=[pl.BlockSpec(memory_space=pltpu.VMEM), pl.BlockSpec(memory_space=pl.ANY)],
+        out_specs=[pl.BlockSpec(memory_space=pl.ANY)] * 2,
+        out_shape=[
+            jax.ShapeDtypeStruct((dp, groups, kinds, half, feats), partial.dtype),
+            jax.ShapeDtypeStruct((groups, kinds, half, width), partial.dtype),
+        ],
+        scratch_shapes=[dma, dma((2, groups)), dma((2, groups)), dma((groups,)), dma((groups,))],
+        cost_estimate=COMM_COST,
         compiler_params=pltpu.CompilerParams(collective_id=2, has_side_effects=True),
         name="send_back",
-    )(partial)
+    )(partial, gathered)
 
 
 def hidden_kernel(a, w, out, total):
@@ -453,19 +517,19 @@
     own, kv, win = spread(
         (query, d_query, residual, d_residual, key, value, d_key, d_value), w_in, groups
     )
+    win, w_out_layer = lax.optimization_barrier((win, w_out_layer))
     w_in_layer = in_layer(win, dp, seq).reshape((dp, INNER) + win.shape)
-    mixed = attend_wide(own, kv, dp)
-    block = lax.all_to_all(mixed, "dp", split_axis=0, concat_axis=0, tiled=True)
-    gathered = along_line(block, groups)
+    gathered = along_line(attend_wide(own, kv, dp), groups)
     hidden = hidden_layer(gathered.reshape(groups, dp, 2 * groups * half, width), w_in_layer, dp)
     partial = jnp.dot(hidden, w_out_layer, preferred_element_type=jnp.float32).astype(jnp.bfloat16)
-    partial = partial.reshape(2, groups, half, dp * feats).transpose(1, 0, 2, 3)
-    sums = jnp.sum(send_back(partial).astype(jnp.float32), axis=0)
-    g = lax.div(lax.axis_index("seq"), INNER)
-    base = lax.dynamic_index_in_dim(gathered, g, axis=3, keepdims=False)
-    base = base.transpose(2, 3, 1, 0, 4).reshape(2, half, dp * feats)
-    done = (base.astype(jnp.float32) + sums).astype(jnp.bfloat16)
-    out = lax.all_to_all(done, "dp", split_axis=2, concat_axis=1, tiled=True)
+    parts, base_other = send_back(partial.reshape(2, groups, half, dp * feats), gathered)
+    x, g, _ = place(groups)
+    base_own = lax.dynamic_index_in_dim(gathered, g, axis=3, keepdims=False)
+    base_own = lax.dynamic_index_in_dim(base_own, x, axis=1, keepdims=False)
+    base = jnp.stack([jnp.where(x == 0, base_own, base_other), jnp.where(x == 0, base_other, base_own)])
+    base = base.transpose(0, 2, 3, 1, 4).reshape(2, 2, half, feats)
+    total = base.astype(jnp.float32) + jnp.sum(parts.astype(jnp.float32), axis=1)
+    out = total.astype(jnp.bfloat16).transpose(1, 0, 2, 3).reshape(2, rows, feats)
     return (out[0], out[1])
 
 
@@ -473,7 +537,7 @@
     query, w_in = args[0], args[8]
     groups = seq // INNER
     tile = groups * HEAD_DIM
-    if seq % INNER or groups < 2 or groups % dp or query.shape[1] % tile or w_in.shape[1] % tile:
+    if dp != 2 or seq % INNER or groups < 2 or groups % dp or query.shape[1] % tile or w_in.shape[1] % tile:
         return by_rows(*args)
     return by_layers(*args, dp=dp, seq=seq)
 

time: 367 us -> 303 us (0.83); the launches traced: 367 us -> 298 us
  waiting for transfers between devices: 48.9 us -> 0.74 us
  blocking collectives: 13.7 us -> 0 us
  local copies, waits for them, and re-layouts: 12 us -> 2.8 us
  Pallas kernels: 261 us -> 267 us
    all_gather x2, waiting for transfers between devices: 31.3 us -> 0.04 us  [in_layer(): lax.all_gather(block, ('dp', 'seq'), axis_index_groups=layers, axis=0, ti...]
    all_to_all x1 -> x0, waiting for transfers between devices: 16.9 us -> none  [by_layers(): block = lax.all_to_all(mixed, 'dp', split_axis=0, concat_axis=0, tiled=True)]
    all_to_all x1 -> x0, blocking collectives: 13.7 us -> none  [by_layers(): out = lax.all_to_all(done, 'dp', split_axis=2, concat_axis=1, tiled=True)]
    pallas_call x1, Pallas kernels: 55.2 us -> 63.9 us  [along_line(): pl.pallas_call(line_kernel, in_specs=[pl.BlockSpec(memory_space=pltpu.VME...]
  transfers between devices with their start and end apart: 3 -> 2, of which waited for: 2 -> 0; matrix products, arithmetic and copies ran while one was open for 1% -> 0% of each run, Pallas kernels for 23% -> 61%
where the time goes in v3:
time: 303 us; the launch traced here: 298 us
  Pallas kernels  267 us (88%)
  between operations  14.1 us (5%)
  matrix products  10.5 us (3%)
    pallas_call x1, Pallas kernels, spread(): pl.pallas_call(spread_kernel, in_specs=[pl.BlockSpec(memory_space=pltpu.V...  104 us
    pallas_call x1, Pallas kernels, send_back(): pl.pallas_call(return_kernel, in_specs=[pl.BlockSpec(memory_space=pltpu.V...  71.1 us
    pallas_call x1, Pallas kernels, along_line(): pl.pallas_call(line_kernel, in_specs=[pl.BlockSpec(memory_space=pltpu.VME...  63.9 us
    pallas_call x1, Pallas kernels, hidden_layer(): pl.pallas_call(hidden_kernel, grid=(dp, groups), in_specs=[pl.BlockSpec((...  15 us
    pallas_call x1, Pallas kernels, attend_wide(): pl.pallas_call(attend_wide_kernel, grid=(heads,), in_specs=[own_spec(i) f...  13.8 us
    dot_general x1, matrix products, by_layers(): jnp.dot(hidden, w_out_layer, preferred_element_type=jnp.float32)  10.5 us
  transfers between devices with their start and end apart: 2, of which 0 were waited for; matrix products, arithmetic and copies ran while one was open for 0% of the time, Pallas kernels for 61%

profile of v3, /device:TPU:8, one launch (start us, length us, event | category | flops | bytes accessed | tf_op | source)
XLA Modules:
  0.0 297.7 jit_solution(16340481380395812678)
XLA Ops:
  7.2 0.0 all-gather.5.cloned.1.call-start
  7.2 0.7 all-gather.5.cloned.1.call-update
  7.9 0.0 all-gather.7.cloned.1.call-start
  7.9 103.8 %spread.1 = (bf16[4,4,128,384]{3,2,1,0:T(8,128)(2,1)}, bf16[4,4,4,128,384]{4,3,2,1,0:T(8,128)(2,1)}, bf16[4,192,896]{2,1,0:T(8,128)(2,1)}) custom-call(bf16[128,1536]{1,0:T(8,128)(2,1)} %q.1, bf16[128,1536]{1,0:T(8,128)(2,1)} %dq.1, bf16[128,1536]{1,0:T(8,128)(2,1)} %res.1, bf16[128,1536]{1,0:T(8,128)(2,1)} %dres.1, bf16[128,1536]{1,0:T(8,128)(2,1)} %k.1, ...), custom_call_target="tpu_custom_call" | custom-call | flops 99999997952 | bytes 100000000 | tf_op jit(solution)/shard_map/spread/pallas_call | solution.py:221
  111.7 0.0 all-gather.5.cloned.1.call-done
  111.7 0.0 all-gather.7.cloned.1.call-update
  111.8 13.8 %attend_wide.1.mixed = bf16[2,2,4,64,384]{4,3,2,1,0:T(8,128)(2,1)} custom-call(bf16[4,4,128,384]{3,2,1,0:T(8,128)(2,1)} %get-tuple-element.9.q.dq.res.dres, bf16[4,4,128,384]{3,2,1,0:T(8,128)(2,1)} %get-tuple-element.9.q.dq.res.dres, bf16[4,4,128,384]{3,2,1,0:T(8,128)(2,1)} %get-tuple-element.9.q.dq.res.dres, ...), custom_call_target="tpu_custom_call" | custom-call | flops 4831838208 | bytes 6291456 | tf_op jit(solution)/shard_map/attend_wide/pallas_call | solution.py:266
  125.6 63.9 %along_line.1.gathered = bf16[4,2,2,4,64,384]{5,4,3,2,1,0:T(8,128)(2,1)} custom-call(bf16[2,2,4,64,384]{4,3,2,1,0:T(8,128)(2,1)} %attend_wide.1.mixed), custom_call_target="tpu_custom_call" | custom-call | flops 99999997952 | bytes 100000000 | tf_op jit(solution)/shard_map/along_line/pallas_call | solution.py:374
  189.4 0.0 all-gather.7.cloned.1.call-done
  189.5 15.0 %hidden_layer.1 = bf16[512,1792]{1,0:T(8,128)(2,1)} custom-call(bf16[4,2,512,384]{3,2,1,0:T(8,128)(2,1)} %bitcast.27, bf16[2,4,4,192,896]{4,3,2,1,0:T(8,128)(2,1)} %bitcast.28), custom_call_target="tpu_custom_call" | custom-call | flops 5637144576 | bytes 11010048 | tf_op jit(solution)/shard_map/hidden_layer/pallas_call | solution.py:485
  204.4 10.5 %convolution_convert_fusion = bf16[512,3072]{1,0:T(8,128)(2,1)} fusion(bf16[512,1792]{1,0:T(8,128)(2,1)} %hidden_layer.1, bf16[1792,3072]{1,0:T(8,128)(2,1)} %all-gather.5.cloned.1.call-done), kind=kOutput, calls=%fused_computation.1 | convolution fusion | flops 5638717440 | bytes 15990784 | tf_op jit(solution)/shard_map/dot_general | solution.py:524
  214.9 71.1 %send_back.1 = (bf16[2,4,2,64,1536]{4,3,2,1,0:T(8,128)(2,1)}, bf16[4,2,64,384]{3,2,1,0:T(8,128)(2,1)}) custom-call(bf16[2,4,64,3072]{3,2,1,0:T(8,128)(2,1)} %bitcast.29, bf16[4,2,2,4,64,384]{5,4,3,2,1,0:T(8,128)(2,1)} %along_line.1.gathered), custom_call_target="tpu_custom_call" | custom-call | flops 99999997952 | bytes 100000000 | tf_op jit(solution)/shard_map/send_back/pallas_call | solution.py:444
  286.0 1.2 fusion.1
  287.2 0.1 convert_bitcast_fusion
  287.3 0.0 copy-start
  287.3 0.2 copy.14
  287.5 1.7 copy-done
  289.2 0.5 convert_reduce_fusion
  289.7 0.2 fusion
  290.0 0.9 fusion.3
Async XLA Ops:
  7.2 104.6 %all-gather.5.cloned.1.call-start = ((), (), s32[]{:S(2)}) async-start(), calls=%async_computation | async-start | bytes 12386304 | tf_op jit(solution)/shard_map/all_gather | solution.py:509
  7.9 181.6 %all-gather.7.cloned.1.call-start = ((), (), s32[]{:S(2)}) async-start(), calls=%async_computation.1 | async-start | bytes 12386304 | tf_op jit(solution)/shard_map/all_gather | solution.py:509
  287.3 1.9 copy-start
Sparse Core Ops, SparseCore 0:
  9.9 79.4 all-gather.4
  111.9 74.1 all-gather.6

commit v4 on v3

--- a/solution.py
+++ b/solution.py
@@ -122,11 +122,10 @@
 
 
 def spread_kernel(
-    q, dq, res, dres, k, v, dk, dv, w_in, own, kv, win, z_send, z_recv, own_sem,
+    q, dq, res, dres, k, v, dk, dv, own, kv, z_send, z_recv, own_sem,
     p_send, p_recv, y_send, y_recv, f_send, f_recv,
 ):
     groups, width = own.shape[1], own.shape[3]
-    hid = win.shape[2]
     x, g, i = place(groups)
     partner = (x, g * INNER + i + 1 - 2 * lax.rem(i, 2))
     across_i = lax.rem(i + 2, INNER)
@@ -137,16 +136,12 @@
     def piece(j, to):
         if j < 4:
             return (k, v, dk, dv)[j].at[:, pl.ds(pl.multiple_of(to * width, 128), width)]
-        if j < 8:
-            return (q, dq, res, dres)[j - 4].at[:, pl.ds(pl.multiple_of(to * width, 128), width)]
-        return w_in.at[:, pl.ds(pl.multiple_of(to * hid, 128), hid)]
+        return (q, dq, res, dres)[j - 4].at[:, pl.ds(pl.multiple_of(to * width, 128), width)]
 
     def slot(j, source):
         if j < 4:
             return kv.at[i, source, j]
-        if j < 8:
-            return own.at[j - 4, source]
-        return win.at[source]
+        return own.at[j - 4, source]
 
     def over_z(t, j):
         return pltpu.make_async_remote_copy(
@@ -169,12 +164,11 @@
         )
 
     z_copies = {}
-    for order in (range(8), (8,)):
-        for t in range(1, groups):
-            for j in order:
-                z_copies[t, j] = over_z(t, j)
-                z_copies[t, j].start()
-    locals_ = [pltpu.make_async_copy(piece(j, g), slot(j, g), own_sem.at[j]) for j in range(9)]
+    for t in range(1, groups):
+        for j in range(8):
+            z_copies[t, j] = over_z(t, j)
+            z_copies[t, j].start()
+    locals_ = [pltpu.make_async_copy(piece(j, g), slot(j, g), own_sem.at[j]) for j in range(8)]
     for copy in locals_:
         copy.start()
     for copy in locals_:
@@ -213,26 +207,69 @@
             copy.wait_recv()
 
 
-def spread(tensors, w_in, groups):
+def spread(tensors, groups):
     rows, feats = tensors[0].shape
     width = feats // groups
-    deep, hid = w_in.shape[0], w_in.shape[1] // groups
     dma = pltpu.SemaphoreType.DMA
     return pl.pallas_call(
         spread_kernel,
-        in_specs=[pl.BlockSpec(memory_space=pltpu.VMEM)] * 9,
-        out_specs=[pl.BlockSpec(memory_space=pl.ANY)] * 3,
+        in_specs=[pl.BlockSpec(memory_space=pltpu.VMEM)] * 8,
+        out_specs=[pl.BlockSpec(memory_space=pl.ANY)] * 2,
         out_shape=[
             jax.ShapeDtypeStruct((4, groups, rows, width), jnp.bfloat16),
             jax.ShapeDtypeStruct((INNER, groups, 4, rows, width), jnp.bfloat16),
-            jax.ShapeDtypeStruct((groups, deep, hid), jnp.bfloat16),
         ],
-        scratch_shapes=[dma((groups - 1, 9)), dma((groups - 1, 9)), dma((9,))]
+        scratch_shapes=[dma((groups - 1, 8)), dma((groups - 1, 8)), dma((8,))]
         + [dma((groups,)) for _ in range(6)],
         cost_estimate=COMM_COST,
         compiler_params=pltpu.CompilerParams(collective_id=0, has_side_effects=True),
         name="spread",
-    )(*tensors, w_in)
+    )(*tensors)
+
+
+def columns_kernel(w_in, win, own_sem, send, recv):
+    groups, _, hid = win.shape
+    x, g, i = place(groups)
+    rows = [lax.rem(g + t, groups) for t in range(groups)]
+    enter([(x, rows[t] * INNER + i) for t in range(1, groups)])
+
+    def piece(t):
+        return w_in.at[:, pl.ds(pl.multiple_of(rows[t] * hid, 128), hid)]
+
+    copies = [
+        pltpu.make_async_remote_copy(
+            src_ref=piece(t),
+            dst_ref=win.at[g],
+            send_sem=send.at[t - 1],
+            recv_sem=recv.at[t - 1],
+            device_id=(x, rows[t] * INNER + i),
+            device_id_type=MESH,
+        )
+        for t in range(1, groups)
+    ]
+    for copy in copies:
+        copy.start()
+    mine = pltpu.make_async_copy(piece(0), win.at[g], own_sem)
+    mine.start()
+    mine.wait()
+    for copy in copies:
+        copy.wait()
+
+
+def columns(w_in, groups):
+    dma = pltpu.SemaphoreType.DMA
+    return pl.pallas_call(
+        columns_kernel,
+        in_specs=[pl.BlockSpec(memory_space=pltpu.VMEM)],
+        out_specs=pl.BlockSpec(memory_space=pl.ANY),
+        out_shape=jax.ShapeDtypeStruct(
+            (groups, w_in.shape[0], w_in.shape[1] // groups), jnp.bfloat16
+        ),
+        scratch_shapes=[dma, dma((groups - 1,)), dma((groups - 1,))],
+        cost_estimate=COMM_COST,
+        compiler_params=pltpu.CompilerParams(collective_id=3, has_side_effects=True),
+        name="columns",
+    )(w_in)
 
 
 def attend_wide_kernel(q, dq, res, dres, k, v, dk, dv, out):
@@ -383,57 +420,97 @@
     )(mixed)
 
 
-def return_kernel(partial, gathered, out, base, own_sem, send, recv, base_send, base_recv):
-    groups, feats = out.shape[1], out.shape[4]
+def return_kernel(
+    partial, gathered, out, base, theirs, joined, own_sem, p_send, p_recv, send, recv,
+    base_send, base_recv,
+):
+    groups, feats = base.shape[0], out.shape[4]
+    kinds = out.shape[2]
     x, g, i = place(groups)
-    steps = [(d, t) for t in range(groups) for d in range(2) if d or t]
     sides = (x, 1 - x)
-    rows = [lax.rem(g + t, groups) for t in range(groups)]
-    enter([(sides[d], rows[t] * INNER + i) for d, t in steps])
-
-    def piece(d, t):
-        return partial.at[:, rows[t], :, pl.ds(pl.multiple_of(sides[d] * feats, 128), feats)]
-
-    copies = [
-        pltpu.make_async_remote_copy(
-            src_ref=piece(d, t),
-            dst_ref=out.at[x, t],
-            send_sem=send.at[d, t],
-            recv_sem=recv.at[d, t],
-            device_id=(sides[d], rows[t] * INNER + i),
+    near = g + 1 - 2 * lax.rem(g, 2)
+    far = lax.rem(g + 2, groups)
+    near_far = lax.rem(near + 2, groups)
+    ends = (g, near, far)
+    steps = [(d, e) for e in range(3) for d in range(2) if d or e]
+    enter([(sides[d], ends[e] * INNER + i) for d, e in steps])
+
+    def part(d):
+        return pl.ds(pl.multiple_of(sides[d] * feats, 128), feats)
+
+    def remote(src, dst, send_sem, recv_sem, d, row):
+        return pltpu.make_async_remote_copy(
+            src_ref=src,
+            dst_ref=dst,
+            send_sem=send_sem,
+            recv_sem=recv_sem,
+            device_id=(sides[d], row * INNER + i),
             device_id_type=MESH,
         )
-        for d, t in sorted(steps, reverse=True)
+
+    def final(d, e, kind):
+        source = joined.at[kind] if e == 2 else partial.at[kind, ends[e]]
+        return remote(
+            source.at[:, part(d)],
+            out.at[x, e, kind],
+            send.at[d, e, kind],
+            recv.at[d, e, kind],
+            d,
+            ends[e],
+        )
+
+    def arrival(d, e, kind):
+        return remote(
+            partial.at[kind, ends[0], :, part(d)],
+            out.at[sides[d], e, kind],
+            send.at[d, e, kind],
+            recv.at[d, e, kind],
+            d,
+            ends[e],
+        )
+
+    across = [
+        remote(
+            partial.at[kind, near_far], theirs.at[kind], p_send.at[kind], p_recv.at[kind], 0, near
+        )
+        for kind in range(kinds)
     ]
-    for k in range(groups):
-        copies.append(
-            pltpu.make_async_remote_copy(
-                src_ref=gathered.at[k, sides[1], :, g],
-                dst_ref=base.at[k],
-                send_sem=base_send.at[k],
-                recv_sem=base_recv.at[k],
-                device_id=(sides[1], g * INNER + i),
-                device_id_type=MESH,
-            )
-        )
-    for copy in copies:
+    bases = [
+        remote(
+            gathered.at[k, sides[1], :, g], base.at[k], base_send.at[k], base_recv.at[k], 1, g
+        )
+        for k in range(groups)
+    ]
+    sent = [final(1, 0, kind) for kind in range(kinds)]
+    for copy in across + sent + bases:
         copy.start()
-    mine = pltpu.make_async_copy(piece(0, 0), out.at[x, 0], own_sem)
-    mine.start()
-    mine.wait()
-    for copy in copies:
+    mine = [
+        pltpu.make_async_copy(
+            partial.at[kind, g, :, part(0)], out.at[x, 0, kind], own_sem.at[kind]
+        )
+        for kind in range(kinds)
+    ]
+    for copy in mine:
+        copy.start()
+    for kind in range(kinds):
+        across[kind].wait_recv()
+        joined[kind] = (
+            partial[kind, far].astype(jnp.float32) + theirs[kind].astype(jnp.float32)
+        ).astype(jnp.bfloat16)
+        for e in (2, 1):
+            for d in range(2):
+                copy = final(d, e, kind)
+                copy.start()
+                sent.append(copy)
+    for copy in mine:
+        copy.wait()
+    for copy in across + sent:
         copy.wait_send()
-    for d, t in steps:
-        pltpu.make_async_remote_copy(
-            src_ref=piece(d, t),
-            dst_ref=out.at[sides[d], t],
-            send_sem=send.at[d, t],
-            recv_sem=recv.at[d, t],
-            device_id=(sides[d], rows[t] * INNER + i),
-            device_id_type=MESH,
-        ).wait_recv()
-    for copy in copies[len(steps) :]:
-        copy.wait_recv()
+    for kind in range(kinds):
+        for d, e in steps:
+            arrival(d, e, kind).wait_recv()
+    for copy in bases:
+        copy.wait()
 
 
 def send_back(partial, gathered):
@@ -446,10 +523,12 @@
         in_specs=[pl.BlockSpec(memory_space=pltpu.VMEM), pl.BlockSpec(memory_space=pl.ANY)],
         out_specs=[pl.BlockSpec(memory_space=pl.ANY)] * 2,
         out_shape=[
-            jax.ShapeDtypeStruct((dp, groups, kinds, half, feats), partial.dtype),
+            jax.ShapeDtypeStruct((dp, 3, kinds, half, feats), partial.dtype),
             jax.ShapeDtypeStruct((groups, kinds, half, width), partial.dtype),
         ],
-        scratch_shapes=[dma, dma((2, groups)), dma((2, groups)), dma((groups,)), dma((groups,))],
+        scratch_shapes=[pltpu.VMEM((kinds, half, dp * feats), jnp.bfloat16) for _ in range(2)]
+        + [dma((kinds,)) for _ in range(3)]
+        + [dma((2, 3, kinds)), dma((2, 3, kinds)), dma((groups,)), dma((groups,))],
         cost_estimate=COMM_COST,
         compiler_params=pltpu.CompilerParams(collective_id=2, has_side_effects=True),
         name="send_back",
@@ -514,10 +593,9 @@
     rows, feats = query.shape
     half, width = rows // dp, feats // groups
     w_out_layer = in_layer(w_out, dp, seq).reshape(dp * INNER * w_out.shape[0], w_out.shape[1])
-    own, kv, win = spread(
-        (query, d_query, residual, d_residual, key, value, d_key, d_value), w_in, groups
-    )
-    win, w_out_layer = lax.optimization_barrier((win, w_out_layer))
+    tensors = (query, d_query, residual, d_residual, key, value, d_key, d_value)
+    win, tensors = lax.optimization_barrier((columns(w_in, groups), tensors))
+    own, kv = spread(tensors, groups)
     w_in_layer = in_layer(win, dp, seq).reshape((dp, INNER) + win.shape)
     gathered = along_line(attend_wide(own, kv, dp), groups)
     hidden = hidden_layer(gathered.reshape(groups, dp, 2 * groups * half, width), w_in_layer, dp)
@@ -537,7 +615,7 @@
     query, w_in = args[0], args[8]
     groups = seq // INNER
     tile = groups * HEAD_DIM
-    if dp != 2 or seq % INNER or groups < 2 or groups % dp or query.shape[1] % tile or w_in.shape[1] % tile:
+    if dp != 2 or seq % INNER or groups != 4 or query.shape[1] % tile or w_in.shape[1] % tile:
         return by_rows(*args)
     return by_layers(*args, dp=dp, seq=seq)
 

time: 303 us -> 312 us (1.030)
  Pallas kernels: 267 us -> 279 us
    pallas_call x0 -> x1, Pallas kernels: none -> 34.5 us  [columns(): pl.pallas_call(columns_kernel, in_specs=[pl.BlockSpec(memory_space=pltpu....]
    pallas_call x1, Pallas kernels: 104 us -> 86.6 us  [spread(): pl.pallas_call(spread_kernel, in_specs=[pl.BlockSpec(memory_space=pltpu.V...]
    pallas_call x1, Pallas kernels: 71.1 us -> 56.9 us  [send_back(): pl.pallas_call(return_kernel, in_specs=[pl.BlockSpec(memory_space=pltpu.V...]
    pallas_call x1, Pallas kernels: 63.9 us -> 71.9 us  [along_line(): pl.pallas_call(line_kernel, in_specs=[pl.BlockSpec(memory_space=pltpu.VME...]
where the time goes in v4:
time: 312 us; the launch traced here: 308 us
  Pallas kernels  279 us (89%)
  between operations  14.1 us (5%)
  matrix products  10.5 us (3%)
    pallas_call x1, Pallas kernels, spread(): pl.pallas_call(spread_kernel, in_specs=[pl.BlockSpec(memory_space=pltpu.V...  86.6 us
    pallas_call x1, Pallas kernels, along_line(): pl.pallas_call(line_kernel, in_specs=[pl.BlockSpec(memory_space=pltpu.VME...  71.9 us
    pallas_call x1, Pallas kernels, send_back(): pl.pallas_call(return_kernel, in_specs=[pl.BlockSpec(memory_space=pltpu.V...  56.9 us
    pallas_call x1, Pallas kernels, columns(): pl.pallas_call(columns_kernel, in_specs=[pl.BlockSpec(memory_space=pltpu....  34.5 us
    pallas_call x1, Pallas kernels, hidden_layer(): pl.pallas_call(hidden_kernel, grid=(dp, groups), in_specs=[pl.BlockSpec((...  15 us
    pallas_call x1, Pallas kernels, attend_wide(): pl.pallas_call(attend_wide_kernel, grid=(heads,), in_specs=[own_spec(i) f...  13.8 us
    dot_general x1, matrix products, by_layers(): jnp.dot(hidden, w_out_layer, preferred_element_type=jnp.float32)  10.5 us
  transfers between devices with their start and end apart: 2, of which 0 were waited for; matrix products, arithmetic and copies ran while one was open for 0% of the time, Pallas kernels for 61%

profile of v4, /device:TPU:8, one launch (start us, length us, event | category | flops | bytes accessed | tf_op | source)
XLA Modules:
  0.0 308.4 jit_solution(16183868516145261897)
XLA Ops:
  7.2 0.0 all-gather.5.cloned.1.call-start
  7.2 34.5 %columns.1 = bf16[4,192,896]{2,1,0:T(8,128)(2,1)} custom-call(bf16[192,3584]{1,0:T(8,128)(2,1)} %w_in.1), custom_call_target="tpu_custom_call" | custom-call | flops 99999997952 | bytes 100000000 | tf_op jit(solution)/shard_map/columns/pallas_call | solution.py:261
  41.7 0.0 all-gather.5.cloned.1.call-update
  41.7 0.0 all-gather.7.cloned.1.call-start
  41.8 0.7 all-gather.7.cloned.1.call-update
  42.5 86.6 %spread.1 = (bf16[4,4,128,384]{3,2,1,0:T(8,128)(2,1)}, bf16[4,4,4,128,384]{4,3,2,1,0:T(8,128)(2,1)}) custom-call(bf16[128,1536]{1,0:T(8,128)(2,1)} %q, bf16[128,1536]{1,0:T(8,128)(2,1)} %dq, bf16[128,1536]{1,0:T(8,128)(2,1)} %res, bf16[128,1536]{1,0:T(8,128)(2,1)} %dres, bf16[128,1536]{1,0:T(8,128)(2,1)} %k, bf16[128,1536]{1,0:T(8,128)(2,1)} %v, ...), custom_call_target="tpu_custom_call" | custom-call | flops 99999997952 | bytes 100000000 | tf_op jit(solution)/shard_map/spread/pallas_call | solution.py:214
  129.1 13.8 %attend_wide.1.mixed = bf16[2,2,4,64,384]{4,3,2,1,0:T(8,128)(2,1)} custom-call(bf16[4,4,128,384]{3,2,1,0:T(8,128)(2,1)} %get-tuple-element.23.q.dq.res.dres, bf16[4,4,128,384]{3,2,1,0:T(8,128)(2,1)} %get-tuple-element.23.q.dq.res.dres, bf16[4,4,128,384]{3,2,1,0:T(8,128)(2,1)} %get-tuple-element.23.q.dq.res.dres, ...), custom_call_target="tpu_custom_call" | custom-call | flops 4831838208 | bytes 6291456 | tf_op jit(solution)/shard_map/attend_wide/pallas_call | solution.py:303
  142.9 71.9 %along_line.1.gathered = bf16[4,2,2,4,64,384]{5,4,3,2,1,0:T(8,128)(2,1)} custom-call(bf16[2,2,4,64,384]{4,3,2,1,0:T(8,128)(2,1)} %attend_wide.1.mixed), custom_call_target="tpu_custom_call" | custom-call | flops 99999997952 | bytes 100000000 | tf_op jit(solution)/shard_map/along_line/pallas_call | solution.py:411
  214.7 0.0 all-gather.5.cloned.1.call-done
  214.8 15.0 %hidden_layer.1 = bf16[512,1792]{1,0:T(8,128)(2,1)} custom-call(bf16[4,2,512,384]{3,2,1,0:T(8,128)(2,1)} %bitcast.27, bf16[2,4,4,192,896]{4,3,2,1,0:T(8,128)(2,1)} %bitcast.28), custom_call_target="tpu_custom_call" | custom-call | flops 5637144576 | bytes 11010048 | tf_op jit(solution)/shard_map/hidden_layer/pallas_call | solution.py:564
  229.7 0.0 all-gather.7.cloned.1.call-done
  229.7 10.5 %convolution_convert_fusion = bf16[512,3072]{1,0:T(8,128)(2,1)} fusion(bf16[512,1792]{1,0:T(8,128)(2,1)} %hidden_layer.1, bf16[1792,3072]{1,0:T(8,128)(2,1)} %all-gather.7.cloned.1.call-done), kind=kOutput, calls=%fused_computation.1 | convolution fusion | flops 5638717440 | bytes 15990784 | tf_op jit(solution)/shard_map/dot_general | solution.py:602
  240.2 56.9 %send_back.1 = (bf16[2,3,2,64,1536]{4,3,2,1,0:T(8,128)(2,1)}, bf16[4,2,64,384]{3,2,1,0:T(8,128)(2,1)}) custom-call(bf16[2,4,64,3072]{3,2,1,0:T(8,128)(2,1)} %bitcast.29, bf16[4,2,2,4,64,384]{5,4,3,2,1,0:T(8,128)(2,1)} %along_line.1.gathered), custom_call_target="tpu_custom_call" | custom-call | flops 99999997952 | bytes 100000000 | tf_op jit(solution)/shard_map/send_back/pallas_call | solution.py:521
  297.1 1.2 fusion.1
  298.3 0.1 convert_bitcast_fusion
  298.4 0.0 copy-start
  298.4 0.2 copy.14
  298.6 1.5 copy-done
  300.1 0.4 convert_reduce_fusion
  300.4 0.2 fusion
  300.7 0.9 fusion.3
Async XLA Ops:
  7.2 207.6 %all-gather.5.cloned.1.call-start = ((), (), s32[]{:S(2)}) async-start(), calls=%async_computation | async-start | bytes 12386304 | tf_op jit(solution)/shard_map/all_gather | solution.py:588
  41.7 188.0 %all-gather.7.cloned.1.call-start = ((), (), s32[]{:S(2)}) async-start(), calls=%async_computation.1 | async-start | bytes 12386304 | tf_op jit(solution)/shard_map/all_gather | solution.py:588
  298.4 1.7 copy-start
Sparse Core Ops, SparseCore 0:
  41.9 88.0 all-gather.4
  131.8 77.8 all-gather.6

commit v5 on v4

--- a/solution.py
+++ b/solution.py
@@ -122,10 +122,11 @@
 
 
 def spread_kernel(
-    q, dq, res, dres, k, v, dk, dv, own, kv, z_send, z_recv, own_sem,
+    q, dq, res, dres, k, v, dk, dv, w_in, own, kv, win, z_send, z_recv, own_sem,
     p_send, p_recv, y_send, y_recv, f_send, f_recv,
 ):
     groups, width = own.shape[1], own.shape[3]
+    hid = win.shape[2]
     x, g, i = place(groups)
     partner = (x, g * INNER + i + 1 - 2 * lax.rem(i, 2))
     across_i = lax.rem(i + 2, INNER)
@@ -136,12 +137,16 @@
     def piece(j, to):
         if j < 4:
             return (k, v, dk, dv)[j].at[:, pl.ds(pl.multiple_of(to * width, 128), width)]
-        return (q, dq, res, dres)[j - 4].at[:, pl.ds(pl.multiple_of(to * width, 128), width)]
+        if j < 8:
+            return (q, dq, res, dres)[j - 4].at[:, pl.ds(pl.multiple_of(to * width, 128), width)]
+        return w_in.at[:, pl.ds(pl.multiple_of(to * hid, 128), hid)]
 
     def slot(j, source):
         if j < 4:
             return kv.at[i, source, j]
-        return own.at[j - 4, source]
+        if j < 8:
+            return own.at[j - 4, source]
+        return win.at[source]
 
     def over_z(t, j):
         return pltpu.make_async_remote_copy(
@@ -164,11 +169,12 @@
         )
 
     z_copies = {}
-    for t in range(1, groups):
-        for j in range(8):
-            z_copies[t, j] = over_z(t, j)
-            z_copies[t, j].start()
-    locals_ = [pltpu.make_async_copy(piece(j, g), slot(j, g), own_sem.at[j]) for j in range(8)]
+    for order in (range(8), (8,)):
+        for t in range(1, groups):
+            for j in order:
+                z_copies[t, j] = over_z(t, j)
+                z_copies[t, j].start()
+    locals_ = [pltpu.make_async_copy(piece(j, g), slot(j, g), own_sem.at[j]) for j in range(9)]
     for copy in locals_:
         copy.start()
     for copy in locals_:
@@ -207,69 +213,26 @@
             copy.wait_recv()
 
 
-def spread(tensors, groups):
+def spread(tensors, w_in, groups):
     rows, feats = tensors[0].shape
     width = feats // groups
+    deep, hid = w_in.shape[0], w_in.shape[1] // groups
     dma = pltpu.SemaphoreType.DMA
     return pl.pallas_call(
         spread_kernel,
-        in_specs=[pl.BlockSpec(memory_space=pltpu.VMEM)] * 8,
-        out_specs=[pl.BlockSpec(memory_space=pl.ANY)] * 2,
+        in_specs=[pl.BlockSpec(memory_space=pltpu.VMEM)] * 9,
+        out_specs=[pl.BlockSpec(memory_space=pl.ANY)] * 3,
         out_shape=[
             jax.ShapeDtypeStruct((4, groups, rows, width), jnp.bfloat16),
             jax.ShapeDtypeStruct((INNER, groups, 4, rows, width), jnp.bfloat16),
+            jax.ShapeDtypeStruct((groups, deep, hid), jnp.bfloat16),
         ],
-        scratch_shapes=[dma((groups - 1, 8)), dma((groups - 1, 8)), dma((8,))]
+        scratch_shapes=[dma((groups - 1, 9)), dma((groups - 1, 9)), dma((9,))]
         + [dma((groups,)) for _ in range(6)],
         cost_estimate=COMM_COST,
         compiler_params=pltpu.CompilerParams(collective_id=0, has_side_effects=True),
         name="spread",
-    )(*tensors)
-
-
-def columns_kernel(w_in, win, own_sem, send, recv):
-    groups, _, hid = win.shape
-    x, g, i = place(groups)
-    rows = [lax.rem(g + t, groups) for t in range(groups)]
-    enter([(x, rows[t] * INNER + i) for t in range(1, groups)])
-
-    def piece(t):
-        return w_in.at[:, pl.ds(pl.multiple_of(rows[t] * hid, 128), hid)]
-
-    copies = [
-        pltpu.make_async_remote_copy(
-            src_ref=piece(t),
-            dst_ref=win.at[g],
-            send_sem=send.at[t - 1],
-            recv_sem=recv.at[t - 1],
-            device_id=(x, rows[t] * INNER + i),
-            device_id_type=MESH,
-        )
-        for t in range(1, groups)
-    ]
-    for copy in copies:
-        copy.start()
-    mine = pltpu.make_async_copy(piece(0), win.at[g], own_sem)
-    mine.start()
-    mine.wait()
-    for copy in copies:
-        copy.wait()
-
-
-def columns(w_in, groups):
-    dma = pltpu.SemaphoreType.DMA
-    return pl.pallas_call(
-        columns_kernel,
-        in_specs=[pl.BlockSpec(memory_space=pltpu.VMEM)],
-        out_specs=pl.BlockSpec(memory_space=pl.ANY),
-        out_shape=jax.ShapeDtypeStruct(
-            (groups, w_in.shape[0], w_in.shape[1] // groups), jnp.bfloat16
-        ),
-        scratch_shapes=[dma, dma((groups - 1,)), dma((groups - 1,))],
-        cost_estimate=COMM_COST,
-        compiler_params=pltpu.CompilerParams(collective_id=3, has_side_effects=True),
-        name="columns",
-    )(w_in)
+    )(*tensors, w_in)
 
 
 def attend_wide_kernel(q, dq, res, dres, k, v, dk, dv, out):
@@ -593,9 +556,10 @@
     rows, feats = query.shape
     half, width = rows // dp, feats // groups
     w_out_layer = in_layer(w_out, dp, seq).reshape(dp * INNER * w_out.shape[0], w_out.shape[1])
-    tensors = (query, d_query, residual, d_residual, key, value, d_key, d_value)
-    win, tensors = lax.optimization_barrier((columns(w_in, groups), tensors))
-    own, kv = spread(tensors, groups)
+    own, kv, win = spread(
+        (query, d_query, residual, d_residual, key, value, d_key, d_value), w_in, groups
+    )
+    win, w_out_layer = lax.optimization_barrier((win, w_out_layer))
     w_in_layer = in_layer(win, dp, seq).reshape((dp, INNER) + win.shape)
     gathered = along_line(attend_wide(own, kv, dp), groups)
     hidden = hidden_layer(gathered.reshape(groups, dp, 2 * groups * half, width), w_in_layer, dp)

time: 312 us -> 285 us (0.913)
  Pallas kernels: 279 us -> 253 us
    pallas_call x1 -> x0, Pallas kernels: 34.5 us -> none  [columns(): pl.pallas_call(columns_kernel, in_specs=[pl.BlockSpec(memory_space=pltpu....]
    pallas_call x1, Pallas kernels: 86.6 us -> 104 us  [spread(): pl.pallas_call(spread_kernel, in_specs=[pl.BlockSpec(memory_space=pltpu.V...]
    pallas_call x1, Pallas kernels: 71.9 us -> 63.9 us  [along_line(): pl.pallas_call(line_kernel, in_specs=[pl.BlockSpec(memory_space=pltpu.VME...]
  transfers between devices with their start and end apart: 2 -> 2, of which waited for: 0 -> 0; matrix products, arithmetic and copies ran while one was open for 0% -> 0% of each run, Pallas kernels for 61% -> 64%
where the time goes in v5:
time: 285 us; the launch traced here: 283 us
  Pallas kernels  253 us (89%)
  between operations  14.1 us (5%)
  matrix products  10.5 us (4%)
    pallas_call x1, Pallas kernels, spread(): pl.pallas_call(spread_kernel, in_specs=[pl.BlockSpec(memory_space=pltpu.V...  104 us
    pallas_call x1, Pallas kernels, along_line(): pl.pallas_call(line_kernel, in_specs=[pl.BlockSpec(memory_space=pltpu.VME...  63.9 us
    pallas_call x1, Pallas kernels, send_back(): pl.pallas_call(return_kernel, in_specs=[pl.BlockSpec(memory_space=pltpu.V...  56.3 us
    pallas_call x1, Pallas kernels, hidden_layer(): pl.pallas_call(hidden_kernel, grid=(dp, groups), in_specs=[pl.BlockSpec((...  15 us
    pallas_call x1, Pallas kernels, attend_wide(): pl.pallas_call(attend_wide_kernel, grid=(heads,), in_specs=[own_spec(i) f...  13.8 us
    dot_general x1, matrix products, by_layers(): jnp.dot(hidden, w_out_layer, preferred_element_type=jnp.float32)  10.5 us
  transfers between devices with their start and end apart: 2, of which 0 were waited for; matrix products, arithmetic and copies ran while one was open for 0% of the time, Pallas kernels for 64%

profile of v5, /device:TPU:8, one launch (start us, length us, event | category | flops | bytes accessed | tf_op | source)
XLA Modules:
  0.0 282.6 jit_solution(310462068535036300)
XLA Ops:
  7.2 0.0 all-gather.5.cloned.1.call-start
  7.2 0.7 all-gather.5.cloned.1.call-update
  7.9 0.0 all-gather.7.cloned.1.call-start
  7.9 103.8 %spread.1 = (bf16[4,4,128,384]{3,2,1,0:T(8,128)(2,1)}, bf16[4,4,4,128,384]{4,3,2,1,0:T(8,128)(2,1)}, bf16[4,192,896]{2,1,0:T(8,128)(2,1)}) custom-call(bf16[128,1536]{1,0:T(8,128)(2,1)} %q.1, bf16[128,1536]{1,0:T(8,128)(2,1)} %dq.1, bf16[128,1536]{1,0:T(8,128)(2,1)} %res.1, bf16[128,1536]{1,0:T(8,128)(2,1)} %dres.1, bf16[128,1536]{1,0:T(8,128)(2,1)} %k.1, ...), custom_call_target="tpu_custom_call" | custom-call | flops 99999997952 | bytes 100000000 | tf_op jit(solution)/shard_map/spread/pallas_call | solution.py:221
  111.7 0.0 all-gather.5.cloned.1.call-done
  111.7 0.0 all-gather.7.cloned.1.call-update
  111.8 13.8 %attend_wide.1.mixed = bf16[2,2,4,64,384]{4,3,2,1,0:T(8,128)(2,1)} custom-call(bf16[4,4,128,384]{3,2,1,0:T(8,128)(2,1)} %get-tuple-element.9.q.dq.res.dres, bf16[4,4,128,384]{3,2,1,0:T(8,128)(2,1)} %get-tuple-element.9.q.dq.res.dres, bf16[4,4,128,384]{3,2,1,0:T(8,128)(2,1)} %get-tuple-element.9.q.dq.res.dres, ...), custom_call_target="tpu_custom_call" | custom-call | flops 4831838208 | bytes 6291456 | tf_op jit(solution)/shard_map/attend_wide/pallas_call | solution.py:266
  125.6 63.9 %along_line.1.gathered = bf16[4,2,2,4,64,384]{5,4,3,2,1,0:T(8,128)(2,1)} custom-call(bf16[2,2,4,64,384]{4,3,2,1,0:T(8,128)(2,1)} %attend_wide.1.mixed), custom_call_target="tpu_custom_call" | custom-call | flops 99999997952 | bytes 100000000 | tf_op jit(solution)/shard_map/along_line/pallas_call | solution.py:374
  189.4 0.0 all-gather.7.cloned.1.call-done
  189.5 15.0 %hidden_layer.1 = bf16[512,1792]{1,0:T(8,128)(2,1)} custom-call(bf16[4,2,512,384]{3,2,1,0:T(8,128)(2,1)} %bitcast.27, bf16[2,4,4,192,896]{4,3,2,1,0:T(8,128)(2,1)} %bitcast.28), custom_call_target="tpu_custom_call" | custom-call | flops 5637144576 | bytes 11010048 | tf_op jit(solution)/shard_map/hidden_layer/pallas_call | solution.py:527
  204.4 10.5 %convolution_convert_fusion = bf16[512,3072]{1,0:T(8,128)(2,1)} fusion(bf16[512,1792]{1,0:T(8,128)(2,1)} %hidden_layer.1, bf16[1792,3072]{1,0:T(8,128)(2,1)} %all-gather.5.cloned.1.call-done), kind=kOutput, calls=%fused_computation.1 | convolution fusion | flops 5638717440 | bytes 15990784 | tf_op jit(solution)/shard_map/dot_general | solution.py:566
  214.9 56.3 %send_back.1 = (bf16[2,3,2,64,1536]{4,3,2,1,0:T(8,128)(2,1)}, bf16[4,2,64,384]{3,2,1,0:T(8,128)(2,1)}) custom-call(bf16[2,4,64,3072]{3,2,1,0:T(8,128)(2,1)} %bitcast.29, bf16[4,2,2,4,64,384]{5,4,3,2,1,0:T(8,128)(2,1)} %along_line.1.gathered), custom_call_target="tpu_custom_call" | custom-call | flops 99999997952 | bytes 100000000 | tf_op jit(solution)/shard_map/send_back/pallas_call | solution.py:484
  271.2 1.2 fusion.1
  272.4 0.1 convert_bitcast_fusion
  272.5 0.0 copy-start
  272.5 0.2 copy.14
  272.7 1.5 copy-done
  274.2 0.4 convert_reduce_fusion
  274.6 0.2 fusion
  274.8 0.9 fusion.3
Async XLA Ops:
  7.2 104.6 %all-gather.5.cloned.1.call-start = ((), (), s32[]{:S(2)}) async-start(), calls=%async_computation | async-start | bytes 12386304 | tf_op jit(solution)/shard_map/all_gather | solution.py:551
  7.9 181.6 %all-gather.7.cloned.1.call-start = ((), (), s32[]{:S(2)}) async-start(), calls=%async_computation.1 | async-start | bytes 12386304 | tf_op jit(solution)/shard_map/all_gather | solution.py:551
  272.5 1.7 copy-start
Sparse Core Ops, SparseCore 0:
  9.9 79.4 all-gather.4
  111.9 74.1 all-gather.6
